TPU v7x, 32 devices: a whole 2x2x4 slice. The times are simulated.
32 devices in a mesh: grp: 2 (over x), wide: 16 (over z, y, core).
Axes of the slice: x: 2, y: 2, z: 4, core: 2. Of those that a mesh axis runs over, the one named last changes fastest.
Arguments:
- hidden: bfloat16 [32, 256, 8192], P(('grp', 'wide')), parts along dimension 0, may hold values from -6 to 6
- output_gradient: bfloat16 [32, 256, 8192], P(('grp', 'wide')), parts along dimension 0, may hold values from -6 to 6
- adapter_up_factor: bfloat16 [8192, 64], replicated, may hold values from -0.0625 to 0.0625
- first_moment_estimate: float32 [64, 8192], P(None, 'wide'), may hold values from -0.06 to 0.06
- second_moment_estimate: float32 [64, 8192], P(None, 'wide'), may hold values from 0.0001 to 0.01
- lengths: int32 [32], P(('grp', 'wide')), parts along dimension 0, may hold values from 32 to 256, as said below
- seeds: int32 [128], P('wide'), may hold values from 0 to 16777215
Outputs:
- features: float32 [32, 4096], P(('grp', 'wide')), parts along dimension 0
There are 2 independent parts, one for each index of `grp`. A program takes and returns all parts, laid end to end along the dimension named above; an argument that names none is the same for every part. Nothing has to cross between parts.
Inputs may be any that keep to these rules, and one draw needn't show every extreme that they name: `lengths`: some sequence has exactly 256 live tokens and some has 32.
All inputs are finite; a program needn't handle non-finite values.
Results may differ from a plain program's by a relative error of at most 0.0039.
Values may be sent and summed in bfloat16 or wider, within the bound.
No kernel may reach another device: no remote copies, remote signals or barrier semaphores. Data moves between devices by JAX's collectives and lax.ppermute only.
A program may use at most 384 MiB of HBM per device.

v0:
```python
import jax
import jax.numpy as jnp
from jax import lax
from jax.sharding import PartitionSpec as P

K = 4096
CB = 64
RB = 8


def mix_bits(hashed):
    for turn in range(2):
        hashed = hashed & 2147483647
        hashed = hashed ^ jnp.right_shift(hashed, 16)
        hashed = hashed * 73244475
    hashed = hashed & 2147483647
    hashed = hashed ^ jnp.right_shift(hashed, 16)
    return hashed


def build_signs(rank_rows, own_cols, seeds):
    col_blocks = own_cols // CB
    row_groups = rank_rows // RB
    row_ids = lax.broadcasted_iota(jnp.int32, (RB, CB, K), 0)
    col_ids = lax.broadcasted_iota(jnp.int32, (RB, CB, K), 1)
    feat_ids = lax.broadcasted_iota(jnp.int32, (RB, CB, K), 2)

    def fill_step(loop_index, table):
        loop_index = loop_index.astype(jnp.int32)
        col_pos = loop_index // row_groups
        grp_pos = loop_index % row_groups
        param_ids = (grp_pos * RB + row_ids) * CB + col_ids
        hashed = mix_bits(param_ids * 1000003 + feat_ids * 7919 + seeds[col_pos])
        block = (1 - 2 * (hashed & 1)).astype(jnp.bfloat16)
        return lax.dynamic_update_slice(table, block, (grp_pos * RB, col_pos * CB, jnp.int32(0)))

    table = jnp.zeros((rank_rows, own_cols, K), jnp.bfloat16)
    table = lax.fori_loop(0, col_blocks * row_groups, fill_step, table)
    return table.reshape(rank_rows * own_cols, K)


def shards(
    hidden,
    output_gradient,
    adapter_up_factor,
    first_moment_estimate,
    second_moment_estimate,
    lengths,
    seeds,
):
    own_seqs, tok_slots = (hidden.shape[0], hidden.shape[1])
    rank_reduced = jnp.einsum(
        "nuk,kv->nuv", output_gradient, adapter_up_factor, preferred_element_type=jnp.float32
    )
    live_mask = lax.broadcasted_iota(jnp.int32, (own_seqs, tok_slots), 1) < lengths[:, None]
    rank_reduced = jnp.where(live_mask[:, :, None], rank_reduced, 0.0).astype(jnp.bfloat16)
    summed = jnp.einsum("str,std->srd", rank_reduced, hidden, preferred_element_type=jnp.float32)
    seq_grad = (summed / lengths.astype(jnp.float32)[:, None, None]).astype(jnp.bfloat16)
    regrouped = lax.all_to_all(seq_grad, "wide", split_axis=2, concat_axis=0, tiled=True)
    grad_full = regrouped.astype(jnp.float32)
    first_new = 0.9 * first_moment_estimate[None] + 0.1 * grad_full
    second_new = 0.999 * second_moment_estimate[None] + 0.001 * grad_full * grad_full
    update = (first_new / (jnp.sqrt(second_new) + 1e-08)).astype(jnp.bfloat16)
    all_seqs, rank_rows, own_cols = update.shape
    flat_update = update.reshape(all_seqs, rank_rows * own_cols)
    signs = build_signs(rank_rows, own_cols, seeds)
    partial_value = jnp.dot(flat_update, signs, preferred_element_type=jnp.float32)
    totals = lax.psum(partial_value, "wide")
    own_rows = lax.dynamic_slice_in_dim(totals, lax.axis_index("wide") * own_seqs, own_seqs, 0)
    return own_rows * lax.rsqrt(jnp.mean(own_rows * own_rows, axis=1, keepdims=True) + 1e-06)


def solution(mesh):
    placed = (
        P(("grp", "wide"), None, None),
        P(("grp", "wide"), None, None),
        P(),
        P(None, "wide"),
        P(None, "wide"),
        P(("grp", "wide")),
        P("wide"),
    )
    return jax.shard_map(
        shards, mesh=mesh, in_specs=placed, out_specs=P(("grp", "wide"), None), check_vma=False
    )
```

profile of v0, /device:TPU:0, one launch (start us, length us, event | category | flops | bytes accessed | tf_op | source)
XLA Modules:
  0.0 859.6 jit_solution(11713822607061688417)
XLA Ops:
  21.7 45.2 %reduce.1 = bf16[8192,64]{1,0:T(8,128)(2,1)S(1)} reduce(bf16[8192,1,64]{2,1,0:T(2,128)(2,1)} %bitcast.44, bf16[]{:T(256)} %broadcast.116), dimensions={1}, to_apply=%bitcast.32.reduce_sub_computation | reduce | bytes 2097154
  69.1 7.4 all-to-all-start
  76.8 81.1 %broadcast_in_dim.23 = bf16[64,512,4096]{2,1,0:T(8,128)(2,1)} broadcast(bf16[]{:T(256)} %constant.173.clone.1), dimensions={} | broadcast | bytes 268435456 | tf_op jit(solution)/shard_map/broadcast_in_dim | solution.py:37
  157.9 496.9 %while.16 = (s32[]{:T(128)}, bf16[64,512,4096]{2,1,0:T(8,128)(2,1)}, s32[8]{0:T(128)S(1)}, s32[]{:T(128)}, s32[]{:T(128)}, /*index=5*/s32[]{:T(128)}, s32[]{:T(1...) while((s32[]{:T(128)}, bf16[64,512,4096]{2,1,0:T(8,128)(2,1)}, s32[8]{0:T(128)S(1)}, ...), condition=%wide.region_1.2_spmd.clone, body=%wide.region_0.1_spmd.clone.sunk | while | flops 46137368 | bytes 4195198 | solution.py:38
  158.5 7.2 fusion.57
  166.3 7.2 fusion.57
  174.1 7.2 fusion.57
  181.9 7.2 fusion.57
  189.7 7.2 fusion.57
  205.2 7.2 fusion.57
  213.0 7.2 fusion.57
  220.8 7.2 fusion.57
  236.3 7.2 fusion.57
  251.8 7.2 fusion.57
  267.4 7.2 fusion.57
  399.2 7.2 fusion.57
  414.7 7.2 fusion.57
  430.2 7.2 fusion.57
  438.0 7.2 fusion.57
  445.8 7.2 fusion.57
  453.6 7.2 fusion.57
  469.1 7.2 fusion.57
  476.9 7.2 fusion.57
  507.9 7.2 fusion.57
  515.7 7.2 fusion.57
  601.0 7.2 fusion.57
  624.2 7.2 fusion.57
  632.0 7.2 fusion.57
  639.8 7.2 fusion.57
  661.8 8.5 bitcast_convert_fusion
  673.6 84.2 %convolution_bitcast_fusion = f32[16,4096]{1,0:T(8,128)} fusion(bf16[64,512,4096]{2,1,0:T(8,128)(2,1)} %get-tuple-element.162, f32[1,64,16,512]{3,2,1,0:T(8,128)S(1)} %copy.9, f32[64,512]{1,0:T(8,128)S(1)} %get-tuple-element.179, f32[64,512]{1,0:T(8,128)S(1)} %get-tuple-element.180), kind=kOutput, calls=%fused_computation.26 | convolution fusion | flops 4299161600 | bytes 271056896 | tf_op jit(solution)/shard_map/dot_general | solution.py:67
  757.8 91.2 %all-reduce.2.cloned.1.call-done = f32[16,4096]{1,0:T(8,128)} async-done(((f32[16,4096]{1,0:T(8,128)}), f32[16,4096]{1,0:T(8,128)}) %all-reduce.2.cloned.1.call-update) | async-done | bytes 262160 | tf_op jit(solution)/shard_map/psum | solution.py:68
  (124 shorter events, 347.5 us)
Async XLA Ops:
  6.5 1.2 copy-start
  69.1 585.7 %all-to-all-start = ((bf16[16,2,16384]{2,1,0:T(2,128)(2,1)}), bf16[16,2,16384]{2,1,0:T(2,128)(2,1)S(1)}, u32[]{:S(2)}, u32[]{:S(2)}) async-start(bf16[16,2,16384]{2,1,0:T(2,128)(2,1)} %reshape.53), calls=%async_computation | async-start | bytes 2097152 | tf_op jit(solution)/shard_map/all_to_all | solution.py:59
  76.5 772.5 %all-reduce.2.cloned.1.call-start = ((), (), s32[]{:S(2)}) async-start(), calls=%async_computation.1 | async-start | bytes 524288 | tf_op jit(solution)/shard_map/psum | solution.py:68
  76.8 81.1 %copy-start.3 = (s32[8]{0:T(128)S(1)}, s32[8]{0:T(128)}, u32[]{:S(2)}) copy-start(s32[8]{0:T(128)} %param.15) | copy-start | bytes 100
  157.9 496.9 %copy-start.1 = (f32[64,512]{1,0:T(8,128)S(1)}, f32[64,512]{1,0:T(8,128)}, u32[]{:S(2)}) copy-start(f32[64,512]{1,0:T(8,128)} %param.13) | copy-start | bytes 393220
  157.9 496.9 %copy-start.2 = (f32[64,512]{1,0:T(8,128)S(1)}, f32[64,512]{1,0:T(8,128)}, u32[]{:S(2)}) copy-start(f32[64,512]{1,0:T(8,128)} %param.12) | copy-start | bytes 393220
Sparse Core Ops, SparseCore 0:
  758.0 91.0 all-reduce.1
where the time goes:
time: 861 us; the launch traced here: 860 us
  other arithmetic  515 us (60%)
  local copies, waits for them, and re-layouts  140 us (16%)
  waiting for transfers between devices  91.2 us (11%)
  matrix products  90.7 us (11%)
  between operations  14.9 us (2%)
    dynamic_update_slice x64, other arithmetic, fill_step(): lax.dynamic_update_slice(table, block, (grp_pos * RB, col_pos * CB, jnp.i...  459 us
    psum x1, waiting for transfers between devices, shards(): totals = lax.psum(partial_value, 'wide')  91.2 us
    dot_general x1, matrix products, shards(): jnp.dot(flat_update, signs, preferred_element_type=jnp.float32)  84.2 us
    broadcast_in_dim x1, local copies, waits for them, and re-layouts, build_signs(): table = jnp.zeros((rank_rows, own_cols, K), jnp.bfloat16)  81.1 us
    unnamed x1, other arithmetic  45.2 us
    dynamic_slice x64, local copies, waits for them, and re-layouts, fill_step(): hashed = mix_bits(param_ids * 1000003 + feat_ids * 7919 + seeds[col_pos])  38.1 us
  transfers between devices with their start and end apart: 2, of which 1 were waited for; matrix products, arithmetic and copies ran while one was open for 67% of the time, Pallas kernels for 0%

commit v1 on v0

v1 whole, which is shorter than its diff:
```python
import functools
import jax
import jax.numpy as jnp
from jax import lax
from jax.experimental import pallas as pl
from jax.experimental.pallas import tpu as pltpu
from jax.sharding import PartitionSpec as P

K = 4096
CB = 64
MUL = 73244475
TOP = (((MUL + 65536) << 15) + 2**31) % 2**32 - 2**31
LOW31 = 2147483647
ROW = 1000003
FEAT = 7919
AXES = ("grp", "wide")
LANES = 128
KT = 256


def shift_down(bits, places):
    return lax.shift_right_logical(bits, jnp.int32(places))


def sign_bits(hashed):
    hashed = (hashed ^ (shift_down(hashed, 16) & 32767)) * MUL
    hashed = (hashed ^ (shift_down(hashed, 16) & 32767)) * jnp.int32(TOP)
    return hashed < 0


def grad_kernel(lens_ref, up_ref, outg_ref, hid_ref, out_ref, acc_ref, low_ref, *, blocks, groups):
    seq, step = pl.program_id(0), pl.program_id(1)

    @pl.when(step == 0)
    def _():
        acc_ref[...] = jnp.zeros_like(acc_ref)

    @pl.when(step < blocks)
    def _():
        acc_ref[...] += lax.dot_general(
            up_ref[...], outg_ref[0], (((1,), (1,)), ((), ())), preferred_element_type=jnp.float32
        )

    @pl.when(step == blocks - 1)
    def _():
        live = lax.broadcasted_iota(jnp.int32, acc_ref.shape, 1) < lens_ref[seq]
        low_ref[...] = jnp.where(live, acc_ref[...], 0.0).astype(jnp.bfloat16)

    @pl.when(step >= blocks)
    def _():
        summed = jnp.dot(low_ref[...], hid_ref[0], preferred_element_type=jnp.float32)
        grad = (summed / lens_ref[seq].astype(jnp.float32)).astype(jnp.bfloat16)
        rows, cols = out_ref.shape[-2:]
        for grp in range(groups):
            for own in range(out_ref.shape[1]):
                out_ref[grp, own, 0] = grad[grp * rows : (grp + 1) * rows, own * cols : (own + 1) * cols]


def seq_grads(hidden, output_gradient, adapter_up_factor, lengths, groups, wide):
    seqs, toks, width = hidden.shape
    outs, rank = adapter_up_factor.shape
    rows, cols = rank // groups, width // wide
    blk = 1024
    blocks = width // blk
    return pl.pallas_call(
        functools.partial(grad_kernel, blocks=blocks, groups=groups),
        out_shape=jax.ShapeDtypeStruct((groups, wide, seqs, rows, cols), jnp.bfloat16),
        grid_spec=pltpu.PrefetchScalarGridSpec(
            num_scalar_prefetch=1,
            grid=(seqs, 2 * blocks),
            in_specs=[
                pl.BlockSpec((rank, outs // blocks), lambda s, i, n: (0, jnp.minimum(i, blocks - 1))),
                pl.BlockSpec((1, toks, outs // blocks), lambda s, i, n: (s, 0, jnp.minimum(i, blocks - 1))),
                pl.BlockSpec((1, toks, blk), lambda s, i, n: (s, 0, jnp.maximum(i - blocks, 0))),
            ],
            out_specs=pl.BlockSpec(
                (groups, blk // cols, 1, rows, cols), lambda s, i, n: (0, jnp.maximum(i - blocks, 0), s, 0, 0)
            ),
            scratch_shapes=[pltpu.VMEM((rank, toks), jnp.float32), pltpu.VMEM((rank, toks), jnp.bfloat16)],
        ),
        name="seq_grads",
    )(lengths, adapter_up_factor.T, output_gradient, hidden)


def project_kernel(
    seeds_ref, grp_ref, grad_ref, first_ref, second_ref, out_ref, wide_ref, upd_ref, sum_ref, pos_ref, *, per_loop
):
    step = pl.program_id(0)
    seqs, rows, cols = grad_ref.shape
    chunk = upd_ref.shape[2]
    halves = cols // chunk
    parts = chunk // CB

    @pl.when(step == 0)
    def _():
        pos_ref[...] = (
            lax.broadcasted_iota(jnp.int32, pos_ref.shape, 0) * ROW
            + lax.broadcasted_iota(jnp.int32, pos_ref.shape, 1) * FEAT
        )
        first_old = 0.9 * first_ref[...]
        second_old = 0.999 * second_ref[...]

        def update_step(seq, carry):
            grad = grad_ref[seq].astype(jnp.float32)
            first_new = first_old + 0.1 * grad
            second_new = second_old + 0.001 * grad * grad
            update = first_new / (jnp.sqrt(second_new) + 1e-08)
            for lane in range(0, cols, LANES):
                part = update[:, lane : lane + LANES]
                wide_ref[lane // LANES, pl.ds(pl.multiple_of(seq * rows, rows), rows), : part.shape[1]] = part
            return carry

        lax.fori_loop(0, seqs, update_step, 0)
        total = jnp.zeros((seqs, min(LANES, chunk)), jnp.float32)
        for row in range(rows):
            for half in range(halves):
                for lane in range(0, chunk, LANES):
                    upd = wide_ref[(half * chunk + lane) // LANES, pl.ds(row, seqs, stride=rows), :]
                    upd = upd[:, : min(LANES, chunk)].astype(jnp.bfloat16)
                    upd_ref[row * halves + half, :, lane : lane + upd.shape[1]] = upd
                    total += upd.astype(jnp.float32)
        sum_ref[...] = jnp.broadcast_to(jnp.sum(total, axis=1, keepdims=True), sum_ref.shape)

    base = grp_ref[0] * (rows * CB * ROW) + step * (KT * FEAT)

    def chunk_step(pos, acc):
        for sub in range(per_loop):
            entry = pos * per_loop + sub
            row, half = entry // halves, sub % halves
            origin = base + row * (CB * ROW)
            tile = [pos_ref[...] + (origin + seeds_ref[half * parts + part]) for part in range(parts)]
            bits = sign_bits(jnp.concatenate(tile, axis=0) if parts > 1 else tile[0])
            weights = jnp.where(bits, -2.0, 0.0).astype(jnp.bfloat16)
            acc += jnp.dot(upd_ref[entry], weights, preferred_element_type=jnp.float32)
        return acc

    start = jnp.broadcast_to(sum_ref[:, :1], (seqs, KT))
    acc = lax.fori_loop(0, upd_ref.shape[0] // per_loop, chunk_step, start)
    feats = out_ref.shape[0] // seqs
    for part in range(KT // LANES):
        out_ref[pl.ds(step * (KT // LANES) + part, seqs, stride=feats), :] = acc[:, part * LANES : (part + 1) * LANES]


def project(grads, first, second, seeds, grp):
    seqs, rows, cols = grads.shape
    chunk = min(256, cols)
    chunks = rows * cols // chunk
    feats = K // LANES
    return pl.pallas_call(
        functools.partial(project_kernel, per_loop=min(16, chunks)),
        out_shape=jax.ShapeDtypeStruct((seqs * feats, LANES), jnp.float32),
        grid_spec=pltpu.PrefetchScalarGridSpec(
            num_scalar_prefetch=2,
            grid=(K // KT,),
            in_specs=[
                pl.BlockSpec((seqs, rows, cols), lambda i, s, g: (0, 0, 0)),
                pl.BlockSpec((rows, cols), lambda i, s, g: (g[0], 0)),
                pl.BlockSpec((rows, cols), lambda i, s, g: (g[0], 0)),
            ],
            out_specs=pl.BlockSpec((seqs * feats, LANES), lambda i, s, g: (0, 0)),
            scratch_shapes=[
                pltpu.VMEM((pl.cdiv(cols, LANES), seqs * rows, LANES), jnp.float32),
                pltpu.VMEM((chunks, seqs, chunk), jnp.bfloat16),
                pltpu.VMEM((seqs, LANES), jnp.float32),
                pltpu.VMEM((CB, KT), jnp.int32),
            ],
        ),
        name="project",
    )(seeds, grp, grads, first, second)


def shards(
    hidden,
    output_gradient,
    adapter_up_factor,
    first_moment_estimate,
    second_moment_estimate,
    lengths,
    seeds,
):
    groups, wide = lax.axis_size("grp"), lax.axis_size("wide")
    devices = groups * wide
    own_seqs = hidden.shape[0]
    grads = seq_grads(hidden, output_gradient, adapter_up_factor, lengths, groups, wide)
    rows, cols = grads.shape[-2:]
    grads = grads.reshape(devices, own_seqs, rows, cols)
    grads = lax.all_to_all(grads, AXES, 0, 0, tiled=True).reshape(devices * own_seqs, rows, cols)
    grp = lax.axis_index("grp").astype(jnp.int32).reshape(1)
    partial = project(grads, first_moment_estimate, second_moment_estimate, seeds, grp)
    partial = partial.reshape(devices, own_seqs, K // LANES, LANES)
    partial = lax.all_to_all(partial, AXES, 0, 0, tiled=True)
    own_rows = jnp.sum(partial, axis=0)
    scale = lax.rsqrt(jnp.mean(own_rows * own_rows, axis=(1, 2), keepdims=True) + 1e-06)
    return (own_rows * scale).reshape(own_seqs, K)


def solution(mesh):
    placed = (
        P(AXES, None, None),
        P(AXES, None, None),
        P(),
        P(None, "wide"),
        P(None, "wide"),
        P(AXES),
        P("wide"),
    )
    with jax.sharding.use_abstract_mesh(mesh.abstract_mesh):
        return jax.shard_map(shards, mesh=mesh, in_specs=placed, out_specs=P(AXES, None), check_vma=False)
```

time: 861 us -> 172 us (0.20)
  other arithmetic: 515 us -> 1.26 us
  local copies, waits for them, and re-layouts: 140 us -> 0.99 us
  Pallas kernels: 0 us -> 115 us
  matrix products: 90.7 us -> 0 us
  waiting for transfers between devices: 91.2 us -> 27.1 us
  blocking collectives: 0 us -> 18.5 us
  between operations: 14.9 us -> 1.36 us
    dynamic_update_slice x64 -> x0, other arithmetic: 459 us -> none  [fill_step(): lax.dynamic_update_slice(table, block, (grp_pos * RB, col_pos * CB, jnp.i...]
    pallas_call x0 -> x2, Pallas kernels: none -> 115 us  [the longest x1 103 us: project(): pl.pallas_call(functools.partial(project_kernel, per_loop=min(16, chunks)...]
    psum x1 -> x0, waiting for transfers between devices: 91.2 us -> none  [shards(): totals = lax.psum(partial_value, 'wide')]
    dot_general x2 -> x0, matrix products: 90.7 us -> none  [the longest x1 84.2 us: shards(): jnp.dot(flat_update, signs, preferred_element_type=jnp.float32)]
    broadcast_in_dim x1 -> x0, local copies, waits for them, and re-layouts: 81.1 us -> none  [build_signs(): table = jnp.zeros((rank_rows, own_cols, K), jnp.bfloat16)]
    unnamed x1 -> x0, other arithmetic: 45.2 us -> none
    dynamic_slice x64 -> x0, local copies, waits for them, and re-layouts: 38.1 us -> none  [fill_step(): hashed = mix_bits(param_ids * 1000003 + feat_ids * 7919 + seeds[col_pos])]
    all_to_all x1, waiting for transfers between devices: 0.01 us -> 27.1 us  [shards(): lax.all_to_all(grads, AXES, 0, 0, tiled=True)]
  transfers between devices with their start and end apart: 2 -> 1, of which waited for: 1 -> 1; matrix products, arithmetic and copies ran while one was open for 67% -> 0% of each run, Pallas kernels for 0% -> 0%
where the time goes in v1:
time: 172 us; the launch traced here: 171 us
  Pallas kernels  115 us (67%)
  waiting for transfers between devices  27.1 us (16%)
  blocking collectives  18.5 us (11%)
  starting transfers between devices  7.33 us (4%)
    pallas_call x1, Pallas kernels, project(): pl.pallas_call(functools.partial(project_kernel, per_loop=min(16, chunks)...  103 us
    all_to_all x1, waiting for transfers between devices, shards(): lax.all_to_all(grads, AXES, 0, 0, tiled=True)  27.1 us
    all_to_all x1, blocking collectives, shards(): partial = lax.all_to_all(partial, AXES, 0, 0, tiled=True)  18.5 us
    pallas_call x1, Pallas kernels, seq_grads(): pl.pallas_call(functools.partial(grad_kernel, blocks=blocks, groups=group...  12.2 us
    all_to_all x1, starting transfers between devices, shards(): lax.all_to_all(grads, AXES, 0, 0, tiled=True)  7.33 us
  transfers between devices with their start and end apart: 1, of which 1 were waited for; matrix products, arithmetic and copies ran while one was open for 0% of the time, Pallas kernels for 0%

profile of v1, /device:TPU:0, one launch (start us, length us, event | category | flops | bytes accessed | tf_op | source)
XLA Modules:
  0.0 171.4 jit_solution(457690100065014749)
XLA Ops:
  0.7 12.2 %seq_grads.1 = bf16[2,16,1,32,512]{4,3,2,1,0:T(8,128)(2,1)} custom-call(s32[1]{0:T(128)S(6)} %copy.10.lens_ref, bf16[64,8192]{1,0:T(8,128)(2,1)} %bitcast.13, bf16[1,256,8192]{2,1,0:T(8,128)(2,1)} %outg_ref.1, bf16[1,256,8192]{2,1,0:T(8,128)(2,1)} %hid_ref.1), custom_call_target="tpu_custom_call" | custom-call | tf_op jit(solution)/shard_map/seq_grads/pallas_call | solution.py:65
  12.8 7.3 %all-to-all-start = ((bf16[32,1,32,512]{3,2,1,0:T(8,128)(2,1)}), bf16[32,1,32,512]{3,2,1,0:T(8,128)(2,1)S(1)}, u32[]{:S(2)}, u32[]{:S(2)}) async-start(bf16[32,1,32,512]{3,2,1,0:T(8,128)(2,1)} %bitcast.11), calls=%async_computation | async-start | bytes 2097152 | tf_op jit(solution)/shard_map/all_to_all | solution.py:187
  20.1 27.1 %all-to-all-done = bf16[32,1,32,512]{3,2,1,0:T(8,128)(2,1)S(1)} async-done(((bf16[32,1,32,512]{3,2,1,0:T(8,128)(2,1)}), bf16[32,1,32,512]{3,2,1,0:T(8,128)(2,1)S(1)}, u32[]{:S(2)}, u32[]{:S(2)}) %all-to-all-start) | async-done | bytes 1048608 | tf_op jit(solution)/shard_map/all_to_all | solution.py:187
  47.3 0.0 copy-start
  47.3 1.0 copy-done
  48.3 102.7 %project.1 = f32[1024,128]{1,0:T(8,128)} custom-call(s32[8]{0:T(128)} %seeds_ref.1, s32[1]{0:T(128)} %bitcast.grp_ref, bf16[32,32,512]{2,1,0:T(8,128)(2,1)} %bitcast.10, f32[64,512]{1,0:T(8,128)} %first_ref.1, f32[64,512]{1,0:T(8,128)} %second_ref.1), custom_call_target="tpu_custom_call" | custom-call | tf_op jit(solution)/shard_map/project/pallas_call | solution.py:149
  151.0 18.5 %all_to_all.10 = f32[32,1,32,128]{3,2,1,0:T(8,128)S(1)} all-to-all(f32[32,1,32,128]{3,2,1,0:T(8,128)} %bitcast.12), channel_id=1, replica_groups=mesh['grp'=2,'wide'=16] {'grp','wide'}, dimensions={0} | all-to-all | bytes 1048576 | tf_op jit(solution)/shard_map/all_to_all | solution.py:191
  169.5 0.6 multiply_reduce_fusion
  170.8 0.6 broadcast_multiply_fusion
  (1 shorter events, 0.0 us)
Async XLA Ops:
  12.8 34.5 %all-to-all-start = ((bf16[32,1,32,512]{3,2,1,0:T(8,128)(2,1)}), bf16[32,1,32,512]{3,2,1,0:T(8,128)(2,1)S(1)}, u32[]{:S(2)}, u32[]{:S(2)}) async-start(bf16[32,1,32,512]{3,2,1,0:T(8,128)(2,1)} %bitcast.11), calls=%async_computation | async-start | bytes 2097152 | tf_op jit(solution)/shard_map/all_to_all | solution.py:187
  47.3 1.0 copy-start

commit v2 on v1

--- a/solution.py
+++ b/solution.py
@@ -16,6 +16,7 @@
 AXES = ("grp", "wide")
 LANES = 128
 KT = 256
+STRIDE = 3
 
 
 def shift_down(bits, places):
@@ -82,10 +83,72 @@
     )(lengths, adapter_up_factor.T, output_gradient, hidden)
 
 
+def fill_positions(pos_ref):
+    pos_ref[...] = (
+        lax.broadcasted_iota(jnp.int32, pos_ref.shape, 0) * ROW
+        + lax.broadcasted_iota(jnp.int32, pos_ref.shape, 1) * FEAT
+    )
+
+
+def sign_weights(pos_ref, seeds_ref, origin, half, parts):
+    tile = [pos_ref[...] + (origin + seeds_ref[half * parts + part]) for part in range(parts)]
+    bits = sign_bits(jnp.concatenate(tile, axis=0) if parts > 1 else tile[0])
+    return jnp.where(bits, -2.0, 0.0).astype(jnp.bfloat16)
+
+
+def presign_kernel(seeds_ref, grp_ref, out_ref, pos_ref, *, rows, halves):
+    tile, block = pl.program_id(0), pl.program_id(1)
+
+    @pl.when((tile == 0) & (block == 0))
+    def _():
+        fill_positions(pos_ref)
+
+    base = grp_ref[0] * (rows * CB * ROW) + tile * (KT * FEAT)
+    per_block, chunk = out_ref.shape[1:3]
+    for sub in range(per_block):
+        row, half = (block * per_block + sub) // halves, sub % halves
+        out_ref[0, sub] = sign_weights(pos_ref, seeds_ref, base + row * (CB * ROW), half, chunk // CB)
+
+
+def presign(seeds, grp, rows, cols):
+    chunk = min(256, cols)
+    chunks = rows * cols // chunk
+    per_block = min(16, chunks)
+    tiles = K // KT // STRIDE
+    return pl.pallas_call(
+        functools.partial(presign_kernel, rows=rows, halves=cols // chunk),
+        out_shape=jax.ShapeDtypeStruct((tiles, chunks, chunk, KT), jnp.bfloat16),
+        grid_spec=pltpu.PrefetchScalarGridSpec(
+            num_scalar_prefetch=2,
+            grid=(tiles, chunks // per_block),
+            out_specs=pl.BlockSpec((1, per_block, chunk, KT), lambda i, j, s, g: (i, j, 0, 0)),
+            scratch_shapes=[pltpu.VMEM((CB, KT), jnp.int32)],
+        ),
+        cost_estimate=pl.CostEstimate(
+            flops=tiles * rows * cols * KT * 10, bytes_accessed=tiles * rows * cols * KT * 2, transcendentals=0
+        ),
+        name="presign",
+    )(seeds, grp)
+
+
 def project_kernel(
-    seeds_ref, grp_ref, grad_ref, first_ref, second_ref, out_ref, wide_ref, upd_ref, sum_ref, pos_ref, *, per_loop
+    seeds_ref,
+    grp_ref,
+    grad_ref,
+    first_ref,
+    second_ref,
+    held_ref,
+    out_ref,
+    wide_ref,
+    upd_ref,
+    sum_ref,
+    pos_ref,
+    *,
+    per_loop,
 ):
     step = pl.program_id(0)
+    held = step % STRIDE == STRIDE - 1
+    held_tiles = pl.num_programs(0) // STRIDE
     seqs, rows, cols = grad_ref.shape
     chunk = upd_ref.shape[2]
     halves = cols // chunk
@@ -93,10 +156,7 @@
 
     @pl.when(step == 0)
     def _():
-        pos_ref[...] = (
-            lax.broadcasted_iota(jnp.int32, pos_ref.shape, 0) * ROW
-            + lax.broadcasted_iota(jnp.int32, pos_ref.shape, 1) * FEAT
-        )
+        fill_positions(pos_ref)
         first_old = 0.9 * first_ref[...]
         second_old = 0.999 * second_ref[...]
 
@@ -121,27 +181,41 @@
                     total += upd.astype(jnp.float32)
         sum_ref[...] = jnp.broadcast_to(jnp.sum(total, axis=1, keepdims=True), sum_ref.shape)
 
-    base = grp_ref[0] * (rows * CB * ROW) + step * (KT * FEAT)
-
-    def chunk_step(pos, acc):
-        for sub in range(per_loop):
-            entry = pos * per_loop + sub
-            row, half = entry // halves, sub % halves
-            origin = base + row * (CB * ROW)
-            tile = [pos_ref[...] + (origin + seeds_ref[half * parts + part]) for part in range(parts)]
-            bits = sign_bits(jnp.concatenate(tile, axis=0) if parts > 1 else tile[0])
-            weights = jnp.where(bits, -2.0, 0.0).astype(jnp.bfloat16)
-            acc += jnp.dot(upd_ref[entry], weights, preferred_element_type=jnp.float32)
-        return acc
-
+    feats = out_ref.shape[0] // seqs
     start = jnp.broadcast_to(sum_ref[:, :1], (seqs, KT))
-    acc = lax.fori_loop(0, upd_ref.shape[0] // per_loop, chunk_step, start)
-    feats = out_ref.shape[0] // seqs
-    for part in range(KT // LANES):
-        out_ref[pl.ds(step * (KT // LANES) + part, seqs, stride=feats), :] = acc[:, part * LANES : (part + 1) * LANES]
-
-
-def project(grads, first, second, seeds, grp):
+
+    def put(tile, acc):
+        for part in range(KT // LANES):
+            spot = tile * (KT // LANES) + part
+            out_ref[pl.ds(spot, seqs, stride=feats), :] = acc[:, part * LANES : (part + 1) * LANES]
+
+    @pl.when(held)
+    def _():
+        def chunk_step(pos, acc):
+            for sub in range(per_loop):
+                entry = pos * per_loop + sub
+                acc += jnp.dot(upd_ref[entry], held_ref[0, entry], preferred_element_type=jnp.float32)
+            return acc
+
+        put(step // STRIDE, lax.fori_loop(0, upd_ref.shape[0] // per_loop, chunk_step, start))
+
+    @pl.when(jnp.logical_not(held))
+    def _():
+        tile = held_tiles + step - step // STRIDE
+        base = grp_ref[0] * (rows * CB * ROW) + tile * (KT * FEAT)
+
+        def chunk_step(pos, acc):
+            for sub in range(per_loop):
+                entry = pos * per_loop + sub
+                row, half = entry // halves, sub % halves
+                weights = sign_weights(pos_ref, seeds_ref, base + row * (CB * ROW), half, parts)
+                acc += jnp.dot(upd_ref[entry], weights, preferred_element_type=jnp.float32)
+            return acc
+
+        put(tile, lax.fori_loop(0, upd_ref.shape[0] // per_loop, chunk_step, start))
+
+
+def project(grads, first, second, seeds, grp, held):
     seqs, rows, cols = grads.shape
     chunk = min(256, cols)
     chunks = rows * cols // chunk
@@ -153,9 +227,12 @@
             num_scalar_prefetch=2,
             grid=(K // KT,),
             in_specs=[
-                pl.BlockSpec((seqs, rows, cols), lambda i, s, g: (0, 0, 0)),
+                pl.BlockSpec(memory_space=pltpu.VMEM),
                 pl.BlockSpec((rows, cols), lambda i, s, g: (g[0], 0)),
                 pl.BlockSpec((rows, cols), lambda i, s, g: (g[0], 0)),
+                pl.BlockSpec(
+                    (1, chunks, chunk, KT), lambda i, s, g: (jnp.maximum(i - STRIDE + 2, 0) // STRIDE, 0, 0, 0)
+                ),
             ],
             out_specs=pl.BlockSpec((seqs * feats, LANES), lambda i, s, g: (0, 0)),
             scratch_shapes=[
@@ -166,7 +243,7 @@
             ],
         ),
         name="project",
-    )(seeds, grp, grads, first, second)
+    )(seeds, grp, grads, first, second, held)
 
 
 def shards(
@@ -183,10 +260,11 @@
     own_seqs = hidden.shape[0]
     grads = seq_grads(hidden, output_gradient, adapter_up_factor, lengths, groups, wide)
     rows, cols = grads.shape[-2:]
+    grp = lax.axis_index("grp").astype(jnp.int32).reshape(1)
     grads = grads.reshape(devices, own_seqs, rows, cols)
+    held = presign(seeds, grp, rows, cols)
     grads = lax.all_to_all(grads, AXES, 0, 0, tiled=True).reshape(devices * own_seqs, rows, cols)
-    grp = lax.axis_index("grp").astype(jnp.int32).reshape(1)
-    partial = project(grads, first_moment_estimate, second_moment_estimate, seeds, grp)
+    partial = project(grads, first_moment_estimate, second_moment_estimate, seeds, grp, held)
     partial = partial.reshape(devices, own_seqs, K // LANES, LANES)
     partial = lax.all_to_all(partial, AXES, 0, 0, tiled=True)
     own_rows = jnp.sum(partial, axis=0)

time: 172 us -> 164 us (0.953)
  waiting for transfers between devices: 27.1 us -> 0.01 us
  Pallas kernels: 115 us -> 131 us
  blocking collectives: 18.5 us -> 21.7 us
    pallas_call x0 -> x1, Pallas kernels: none -> 33.8 us  [presign(): pl.pallas_call(functools.partial(presign_kernel, rows=rows, halves=cols /...]
    all_to_all x1, waiting for transfers between devices: 27.1 us -> 0.01 us  [shards(): lax.all_to_all(grads, AXES, 0, 0, tiled=True)]
    pallas_call x1, Pallas kernels: 103 us -> 85 us  [project(): pl.pallas_call(functools.partial(project_kernel, per_loop=min(16, chunks)...]
    all_to_all x1, blocking collectives: 18.5 us -> 21.7 us  [shards(): partial = lax.all_to_all(partial, AXES, 0, 0, tiled=True)]
  transfers between devices with their start and end apart: 1 -> 1, of which waited for: 1 -> 0; matrix products, arithmetic and copies ran while one was open for 0% -> 0% of each run, Pallas kernels for 0% -> 21%
where the time goes in v2:
time: 164 us
  Pallas kernels  131 us (80%)
  blocking collectives  21.7 us (13%)
  starting transfers between devices  7.33 us (4%)
    pallas_call x1, Pallas kernels, project(): pl.pallas_call(functools.partial(project_kernel, per_loop=min(16, chunks)...  85 us
    pallas_call x1, Pallas kernels, presign(): pl.pallas_call(functools.partial(presign_kernel, rows=rows, halves=cols /...  33.8 us
    all_to_all x1, blocking collectives, shards(): partial = lax.all_to_all(partial, AXES, 0, 0, tiled=True)  21.7 us
    pallas_call x1, Pallas kernels, seq_grads(): pl.pallas_call(functools.partial(grad_kernel, blocks=blocks, groups=group...  12.2 us
    all_to_all x1, starting transfers between devices, shards(): lax.all_to_all(grads, AXES, 0, 0, tiled=True)  7.33 us
  transfers between devices with their start and end apart: 1, of which 0 were waited for; matrix products, arithmetic and copies ran while one was open for 0% of the time, Pallas kernels for 21%

profile of v2, /device:TPU:0, one launch (start us, length us, event | category | flops | bytes accessed | tf_op | source)
XLA Modules:
  0.0 163.6 jit_solution(14783240850200162165)
XLA Ops:
  0.7 12.2 %seq_grads.1 = bf16[2,16,1,32,512]{4,3,2,1,0:T(8,128)(2,1)} custom-call(s32[1]{0:T(128)S(6)} %copy.10.lens_ref, bf16[64,8192]{1,0:T(8,128)(2,1)} %bitcast.13, bf16[1,256,8192]{2,1,0:T(8,128)(2,1)} %outg_ref.1, bf16[1,256,8192]{2,1,0:T(8,128)(2,1)} %hid_ref.1), custom_call_target="tpu_custom_call" | custom-call | tf_op jit(solution)/shard_map/seq_grads/pallas_call | solution.py:66
  12.8 7.3 %all-to-all-start = ((bf16[32,1,32,512]{3,2,1,0:T(8,128)(2,1)}), bf16[32,1,32,512]{3,2,1,0:T(8,128)(2,1)S(1)}, u32[]{:S(2)}, u32[]{:S(2)}) async-start(bf16[32,1,32,512]{3,2,1,0:T(8,128)(2,1)} %bitcast.11), calls=%async_computation | async-start | bytes 2097152 | tf_op jit(solution)/shard_map/all_to_all | solution.py:266
  20.1 33.8 %presign.1.held_ref = bf16[5,64,256,256]{3,2,1,0:T(8,128)(2,1)} custom-call(s32[8]{0:T(128)} %seeds_ref.3, s32[1]{0:T(128)} %bitcast.grp_ref), custom_call_target="tpu_custom_call" | custom-call | flops 209715200 | bytes 41943040 | tf_op jit(solution)/shard_map/presign/pallas_call | solution.py:118
  54.0 0.0 all-to-all-done
  54.0 0.0 copy-start
  54.0 1.0 copy-done
  55.0 85.0 %project.1 = f32[1024,128]{1,0:T(8,128)} custom-call(s32[8]{0:T(128)} %seeds_ref.3, s32[1]{0:T(128)} %bitcast.grp_ref, bf16[32,32,512]{2,1,0:T(8,128)(2,1)} %bitcast.10, f32[64,512]{1,0:T(8,128)} %first_ref.1, f32[64,512]{1,0:T(8,128)} %second_ref.1, bf16[5,64,256,256]{3,2,1,0:T(8,128)(2,1)} %presign.1.held_ref), custom_call_target="tpu_custom_call" | custom-call | tf_op jit(solution)/shard_map/project/pallas_call | solution.py:223
  140.0 21.7 %all_to_all.10 = f32[32,1,32,128]{3,2,1,0:T(8,128)S(1)} all-to-all(f32[32,1,32,128]{3,2,1,0:T(8,128)} %bitcast.12), channel_id=1, replica_groups=mesh['grp'=2,'wide'=16] {'grp','wide'}, dimensions={0} | all-to-all | bytes 1048576 | tf_op jit(solution)/shard_map/all_to_all | solution.py:269
  161.7 0.6 multiply_reduce_fusion
  163.0 0.6 broadcast_multiply_fusion
  (1 shorter events, 0.0 us)
Async XLA Ops:
  12.8 41.2 %all-to-all-start = ((bf16[32,1,32,512]{3,2,1,0:T(8,128)(2,1)}), bf16[32,1,32,512]{3,2,1,0:T(8,128)(2,1)S(1)}, u32[]{:S(2)}, u32[]{:S(2)}) async-start(bf16[32,1,32,512]{3,2,1,0:T(8,128)(2,1)} %bitcast.11), calls=%async_computation | async-start | bytes 2097152 | tf_op jit(solution)/shard_map/all_to_all | solution.py:266
  54.0 1.0 copy-start

commit v3 on v2

v3 whole, which is shorter than its diff:
```python
import functools
import jax
import jax.numpy as jnp
from jax import lax
from jax.experimental import pallas as pl
from jax.experimental.pallas import tpu as pltpu
from jax.sharding import PartitionSpec as P

K = 4096
CB = 64
MUL = 73244475
TOP = (((MUL + 65536) << 15) + 2**31) % 2**32 - 2**31
LOW31 = 2147483647
ROW = 1000003
FEAT = 7919
AXES = ("grp", "wide")
LANES = 128
KT = 256
SLAB = 128
SLABS = 10
SEQ_BLOCK = 16


def shift_down(bits, places):
    return lax.shift_right_logical(bits, jnp.int32(places))


def mixed(hashed, wraps):
    top = shift_down(hashed, 16)
    if wraps:
        top = top & 32767
    hashed = (hashed ^ top) * MUL
    return (hashed ^ (shift_down(hashed, 16) & 32767)) * jnp.int32(TOP)


def sign_weights(top):
    return jnp.where(top < 0, -2.0, 0.0).astype(jnp.bfloat16)


def grad_kernel(lens_ref, up_any, outg_any, hid_any, out_ref, up_ref, outg_ref, hid_ref, sems):
    seq = pl.program_id(0)
    blocks, toks, outs = outg_ref.shape
    width = hid_ref.shape[2]
    groups, wide, _, rows, cols = out_ref.shape

    def loads(blk):
        return (
            pltpu.make_async_copy(up_any.at[:, pl.ds(blk * outs, outs)], up_ref.at[blk], sems.at[0, blk]),
            pltpu.make_async_copy(outg_any.at[seq, :, pl.ds(blk * outs, outs)], outg_ref.at[blk], sems.at[1, blk]),
            pltpu.make_async_copy(hid_any.at[seq, :, pl.ds(blk * width, width)], hid_ref.at[blk], sems.at[2, blk]),
        )

    copies = [loads(blk) for blk in range(blocks)]
    for load_up, load_outg, _ in copies:
        load_up.start()
        load_outg.start()
    for _, _, load_hid in copies:
        load_hid.start()
    low = jnp.zeros((toks, up_ref.shape[1]), jnp.float32)
    for blk, (load_up, load_outg, _) in enumerate(copies):
        load_up.wait()
        load_outg.wait()
        low += lax.dot_general(
            outg_ref[blk], up_ref[blk], (((1,), (1,)), ((), ())), preferred_element_type=jnp.float32
        )
    live = lax.broadcasted_iota(jnp.int32, low.shape, 0) < lens_ref[seq]
    low = jnp.where(live, low, 0.0).T.astype(jnp.bfloat16)
    count = lens_ref[seq].astype(jnp.float32)
    for blk, (_, _, load_hid) in enumerate(copies):
        load_hid.wait()
        summed = jnp.dot(low, hid_ref[blk], preferred_element_type=jnp.float32)
        grad = (summed / count).astype(jnp.bfloat16)
        for grp in range(groups):
            for own in range(width // cols):
                out_ref[grp, blk * (width // cols) + own, 0] = grad[
                    grp * rows : (grp + 1) * rows, own * cols : (own + 1) * cols
                ]


def seq_grads(hidden, output_gradient, adapter_up_factor, lengths, groups, wide):
    seqs, toks, width = hidden.shape
    outs, rank = adapter_up_factor.shape
    rows, cols = rank // groups, width // wide
    blocks = 4
    return pl.pallas_call(
        grad_kernel,
        out_shape=jax.ShapeDtypeStruct((groups, wide, seqs, rows, cols), jnp.bfloat16),
        grid_spec=pltpu.PrefetchScalarGridSpec(
            num_scalar_prefetch=1,
            grid=(seqs,),
            in_specs=[pl.BlockSpec(memory_space=pl.ANY)] * 3,
            out_specs=pl.BlockSpec((groups, wide, 1, rows, cols), lambda s, n: (0, 0, s, 0, 0)),
            scratch_shapes=[
                pltpu.VMEM((blocks, rank, outs // blocks), jnp.bfloat16),
                pltpu.VMEM((blocks, toks, outs // blocks), jnp.bfloat16),
                pltpu.VMEM((blocks, toks, width // blocks), jnp.bfloat16),
                pltpu.SemaphoreType.DMA((3, blocks)),
            ],
        ),
        name="seq_grads",
    )(lengths, adapter_up_factor.T, output_gradient, hidden)


def fill_positions(pos_ref):
    pos_ref[...] = (
        lax.broadcasted_iota(jnp.int32, pos_ref.shape, 0) * ROW
        + lax.broadcasted_iota(jnp.int32, pos_ref.shape, 1) * FEAT
    )


BLOCK = CB * ROW
SPAN = (CB - 1) * ROW + (K - 1) * FEAT
EDGE = 2**31 - SPAN


def fill_turns(turn_ref, seeds_ref, first_row, rows):
    for pos in range(turn_ref.shape[0]):
        short = EDGE - ((seeds_ref[pos] + first_row * BLOCK) & LOW31)
        turn_ref[pos] = lax.div(jnp.maximum(short + (BLOCK - 1), 0), jnp.int32(BLOCK)) + 2


def slot_row(turn, slot, rows):
    return lax.rem(turn + slot, jnp.int32(rows))


def slot_wraps(slot, rows):
    return slot >= rows - 2 or rows * BLOCK + SPAN > 2**31


def slot_tile(pos_ref, seeds_ref, turn_ref, first_row, feat, slot, half, parts, rows):
    tile = []
    for part in range(half * parts, (half + 1) * parts):
        row = first_row + slot_row(turn_ref[part], slot, rows)
        tile.append(pos_ref[...] + ((seeds_ref[part] + row * BLOCK + feat * FEAT) & LOW31))
    return mixed(jnp.concatenate(tile, axis=0) if parts > 1 else tile[0], slot_wraps(slot, rows))


def presign_kernel(seeds_ref, grp_ref, out_ref, pos_ref, turn_ref, *, rows, halves):
    slab = pl.program_id(0)
    first_row = grp_ref[0] * rows
    pairs, chunk, feats = out_ref.shape[1:]

    @pl.when(slab == 0)
    def _():
        fill_positions(pos_ref)
        fill_turns(turn_ref, seeds_ref, first_row, rows)

    def top_of(entry):
        slot, half = divmod(entry, halves)
        return slot_tile(pos_ref, seeds_ref, turn_ref, first_row, slab * feats, slot, half, chunk // CB, rows)

    for pair in range(pairs):
        out_ref[0, pair] = top_of(2 * pair) | shift_down(top_of(2 * pair + 1), 17)


def presign(seeds, grp, rows, cols):
    chunk = min(256, cols)
    chunks = rows * cols // chunk
    return pl.pallas_call(
        functools.partial(presign_kernel, rows=rows, halves=cols // chunk),
        out_shape=jax.ShapeDtypeStruct((SLABS, chunks // 2, chunk, SLAB), jnp.int32),
        grid_spec=pltpu.PrefetchScalarGridSpec(
            num_scalar_prefetch=2,
            grid=(SLABS,),
            out_specs=pl.BlockSpec((1, chunks // 2, chunk, SLAB), lambda i, s, g: (i, 0, 0, 0)),
            scratch_shapes=[pltpu.VMEM((CB, SLAB), jnp.int32), pltpu.SMEM((cols // CB,), jnp.int32)],
        ),
        cost_estimate=pl.CostEstimate(
            flops=SLABS * SLAB * rows * cols * 10, bytes_accessed=SLABS * SLAB * rows * cols * 2, transcendentals=0
        ),
        name="presign",
    )(seeds, grp)


def project_kernel(
    seeds_ref,
    grp_ref,
    grad_ref,
    first_ref,
    second_ref,
    held_ref,
    out_ref,
    wide_ref,
    upd_ref,
    sum_ref,
    pos_ref,
    turn_ref,
):
    step = pl.program_id(0)
    seqs, rows, cols = grad_ref.shape
    chunk = upd_ref.shape[2]
    halves = cols // chunk
    parts = chunk // CB
    first_row = grp_ref[0] * rows

    @pl.when(step == 0)
    def _():
        fill_positions(pos_ref)
        fill_turns(turn_ref, seeds_ref, first_row, rows)
        width = min(LANES, cols)

        def update_step(blk, carry):
            at = pl.ds(pl.multiple_of(blk * SEQ_BLOCK, SEQ_BLOCK), SEQ_BLOCK)
            for row in range(0, rows, 8):
                for lane in range(0, cols, LANES):
                    spot = (slice(row, row + 8), slice(lane, lane + width))
                    grad = grad_ref[(at, *spot)].astype(jnp.float32)
                    first_new = 0.9 * first_ref[spot] + 0.1 * grad
                    second_new = 0.999 * second_ref[spot] + 0.001 * grad * grad
                    update = first_new / (jnp.sqrt(second_new) + 1e-08)
                    update = jnp.swapaxes(update, 0, 1).astype(jnp.bfloat16)
                    wide_ref[lane // LANES, row : row + 8, at, :width] = update
            return carry

        lax.fori_loop(0, seqs // SEQ_BLOCK, update_step, 0)
        total = jnp.zeros((seqs, width), jnp.float32)
        lanes = lax.broadcasted_iota(jnp.int32, (seqs, LANES), 1)
        for entry in range(upd_ref.shape[0]):
            slot, half = divmod(entry, halves)
            for lane in range(0, chunk, LANES):
                spot = half * chunk + lane
                upd = wide_ref[spot // LANES, slot_row(turn_ref[spot // CB], slot, rows)]
                for pos in range(CB, width, CB):
                    row = slot_row(turn_ref[(spot + pos) // CB], slot, rows)
                    upd = jnp.where(lanes < pos, upd, wide_ref[spot // LANES, row])
                upd = upd[:, :width]
                upd_ref[entry, :, lane : lane + width] = upd
                total += upd.astype(jnp.float32)
        sum_ref[...] = jnp.broadcast_to(jnp.sum(total, axis=1, keepdims=True), sum_ref.shape)

    feats = out_ref.shape[0] // seqs
    held_feats = SLABS * SLAB
    start = jnp.broadcast_to(sum_ref[:, :1], (seqs, KT))

    def put(first_feat, acc):
        for part in range(acc.shape[1] // LANES):
            out_ref[pl.ds(first_feat // LANES + part, seqs, stride=feats), :] = acc[:, part * LANES : (part + 1) * LANES]

    def tile_step(with_held):
        feat = held_feats + step * KT
        acc, held_acc = start, start[:, :SLAB]
        for entry in range(upd_ref.shape[0]):
            slot, half = divmod(entry, halves)
            weights = sign_weights(slot_tile(pos_ref, seeds_ref, turn_ref, first_row, feat, slot, half, parts, rows))
            acc += jnp.dot(upd_ref[entry], weights, preferred_element_type=jnp.float32)
            if with_held:
                top = held_ref[0, entry // 2]
                weights = sign_weights(top << 17 if entry % 2 else top)
                held_acc += jnp.dot(upd_ref[entry], weights, preferred_element_type=jnp.float32)
        put(feat, acc)
        if with_held:
            put(step * SLAB, held_acc)

    pl.when(step < SLABS)(lambda: tile_step(True))
    pl.when(step >= SLABS)(lambda: tile_step(False))


def project(grads, first, second, seeds, grp, held):
    seqs, rows, cols = grads.shape
    chunk = min(256, cols)
    chunks = rows * cols // chunk
    feats = K // LANES
    return pl.pallas_call(
        project_kernel,
        out_shape=jax.ShapeDtypeStruct((seqs * feats, LANES), jnp.float32),
        grid_spec=pltpu.PrefetchScalarGridSpec(
            num_scalar_prefetch=2,
            grid=((K - SLABS * SLAB) // KT,),
            in_specs=[
                pl.BlockSpec(memory_space=pltpu.VMEM),
                pl.BlockSpec((rows, cols), lambda i, s, g: (g[0], 0)),
                pl.BlockSpec((rows, cols), lambda i, s, g: (g[0], 0)),
                pl.BlockSpec((1, chunks // 2, chunk, SLAB), lambda i, s, g: (jnp.minimum(i, SLABS - 1), 0, 0, 0)),
            ],
            out_specs=pl.BlockSpec((seqs * feats, LANES), lambda i, s, g: (0, 0)),
            scratch_shapes=[
                pltpu.VMEM((pl.cdiv(cols, LANES), rows, seqs, LANES), jnp.bfloat16),
                pltpu.VMEM((chunks, seqs, chunk), jnp.bfloat16),
                pltpu.VMEM((seqs, LANES), jnp.float32),
                pltpu.VMEM((CB, KT), jnp.int32),
                pltpu.SMEM((cols // CB,), jnp.int32),
            ],
        ),
        name="project",
    )(seeds, grp, grads, first, second, held)


def shards(
    hidden,
    output_gradient,
    adapter_up_factor,
    first_moment_estimate,
    second_moment_estimate,
    lengths,
    seeds,
):
    groups, wide = lax.axis_size("grp"), lax.axis_size("wide")
    devices = groups * wide
    own_seqs = hidden.shape[0]
    grads = seq_grads(hidden, output_gradient, adapter_up_factor, lengths, groups, wide)
    rows, cols = grads.shape[-2:]
    grp = lax.axis_index("grp").astype(jnp.int32).reshape(1)
    grads = grads.reshape(devices, own_seqs, rows, cols)
    held = presign(seeds, grp, rows, cols)
    grads = lax.all_to_all(grads, AXES, 0, 0, tiled=True).reshape(devices * own_seqs, rows, cols)
    partial = project(grads, first_moment_estimate, second_moment_estimate, seeds, grp, held)
    partial = partial.reshape(devices, own_seqs, K // LANES, LANES)
    partial = lax.all_to_all(partial, AXES, 0, 0, tiled=True)
    own_rows = jnp.sum(partial, axis=0)
    scale = lax.rsqrt(jnp.mean(own_rows * own_rows, axis=(1, 2), keepdims=True) + 1e-06)
    return (own_rows * scale).reshape(own_seqs, K)


def solution(mesh):
    placed = (
        P(AXES, None, None),
        P(AXES, None, None),
        P(),
        P(None, "wide"),
        P(None, "wide"),
        P(AXES),
        P("wide"),
    )
    with jax.sharding.use_abstract_mesh(mesh.abstract_mesh):
        return jax.shard_map(shards, mesh=mesh, in_specs=placed, out_specs=P(AXES, None), check_vma=False)
```

time: 164 us -> 136 us (0.83)
  Pallas kernels: 131 us -> 103 us
    pallas_call x2, Pallas kernels: 97.2 us -> 74.9 us  [the longest x1 68.5 us: project(): pl.pallas_call(project_kernel, out_shape=jax.ShapeDtypeStruct((seqs * fea...]
    pallas_call x1, Pallas kernels: 33.8 us -> 27.7 us  [presign(): pl.pallas_call(functools.partial(presign_kernel, rows=rows, halves=cols /...]
  transfers between devices with their start and end apart: 1 -> 1, of which waited for: 0 -> 0; matrix products, arithmetic and copies ran while one was open for 0% -> 0% of each run, Pallas kernels for 21% -> 20%
where the time goes in v3:
time: 136 us; the launch traced here: 135 us
  Pallas kernels  103 us (76%)
  blocking collectives  21.7 us (16%)
  starting transfers between devices  7.33 us (5%)
  between operations  1.37 us (1%)
    pallas_call x1, Pallas kernels, project(): pl.pallas_call(project_kernel, out_shape=jax.ShapeDtypeStruct((seqs * fea...  68.5 us
    pallas_call x1, Pallas kernels, presign(): pl.pallas_call(functools.partial(presign_kernel, rows=rows, halves=cols /...  27.7 us
    all_to_all x1, blocking collectives, shards(): partial = lax.all_to_all(partial, AXES, 0, 0, tiled=True)  21.7 us
    all_to_all x1, starting transfers between devices, shards(): lax.all_to_all(grads, AXES, 0, 0, tiled=True)  7.33 us
    pallas_call x1, Pallas kernels, seq_grads(): pl.pallas_call(grad_kernel, out_shape=jax.ShapeDtypeStruct((groups, wide,...  6.48 us
  transfers between devices with their start and end apart: 1, of which 0 were waited for; matrix products, arithmetic and copies ran while one was open for 0% of the time, Pallas kernels for 20%

profile of v3, /device:TPU:0, one launch (start us, length us, event | category | flops | bytes accessed | tf_op | source)
XLA Modules:
  0.0 135.3 jit_solution(5031069807939258436)
XLA Ops:
  0.7 6.5 %seq_grads.1 = bf16[2,16,1,32,512]{4,3,2,1,0:T(8,128)(2,1)} custom-call(s32[1]{0:T(128)S(6)} %copy.10.lens_ref, bf16[64,8192]{1,0:T(8,128)(2,1)} %bitcast.13, bf16[1,256,8192]{2,1,0:T(8,128)(2,1)} %outg_any.1, bf16[1,256,8192]{2,1,0:T(8,128)(2,1)} %hid_any.1), custom_call_target="tpu_custom_call" | custom-call | tf_op jit(solution)/shard_map/seq_grads/pallas_call | solution.py:85
  7.1 7.3 %all-to-all-start = ((bf16[32,1,32,512]{3,2,1,0:T(8,128)(2,1)}), bf16[32,1,32,512]{3,2,1,0:T(8,128)(2,1)S(1)}, u32[]{:S(2)}, u32[]{:S(2)}) async-start(bf16[32,1,32,512]{3,2,1,0:T(8,128)(2,1)} %bitcast.11), calls=%async_computation | async-start | bytes 2097152 | tf_op jit(solution)/shard_map/all_to_all | solution.py:305
  14.5 27.7 %presign.1.held_ref = s32[10,32,256,128]{3,2,1,0:T(8,128)} custom-call(s32[8]{0:T(128)} %seeds_ref.3, s32[1]{0:T(128)} %bitcast.grp_ref), custom_call_target="tpu_custom_call" | custom-call | flops 209715200 | bytes 41943040 | tf_op jit(solution)/shard_map/presign/pallas_call | solution.py:159
  42.2 0.0 all-to-all-done
  42.2 0.0 copy-start
  42.2 1.0 copy-done
  43.2 68.5 %project.1 = f32[1024,128]{1,0:T(8,128)} custom-call(s32[8]{0:T(128)} %seeds_ref.3, s32[1]{0:T(128)} %bitcast.grp_ref, bf16[32,32,512]{2,1,0:T(8,128)(2,1)} %bitcast.10, f32[64,512]{1,0:T(8,128)} %first_ref.1, f32[64,512]{1,0:T(8,128)} %second_ref.1, s32[10,32,256,128]{3,2,1,0:T(8,128)} %presign.1.held_ref), custom_call_target="tpu_custom_call" | custom-call | tf_op jit(solution)/shard_map/project/pallas_call | solution.py:263
  111.6 21.7 %all_to_all.10 = f32[32,1,32,128]{3,2,1,0:T(8,128)S(1)} all-to-all(f32[32,1,32,128]{3,2,1,0:T(8,128)} %bitcast.12), channel_id=1, replica_groups=mesh['grp'=2,'wide'=16] {'grp','wide'}, dimensions={0} | all-to-all | bytes 1048576 | tf_op jit(solution)/shard_map/all_to_all | solution.py:308
  133.4 0.6 multiply_reduce_fusion
  134.7 0.6 broadcast_multiply_fusion
  (1 shorter events, 0.0 us)
Async XLA Ops:
  7.1 35.1 %all-to-all-start = ((bf16[32,1,32,512]{3,2,1,0:T(8,128)(2,1)}), bf16[32,1,32,512]{3,2,1,0:T(8,128)(2,1)S(1)}, u32[]{:S(2)}, u32[]{:S(2)}) async-start(bf16[32,1,32,512]{3,2,1,0:T(8,128)(2,1)} %bitcast.11), calls=%async_computation | async-start | bytes 2097152 | tf_op jit(solution)/shard_map/all_to_all | solution.py:305
  42.2 1.0 copy-start

commit v4 on v3

--- a/solution.py
+++ b/solution.py
@@ -17,8 +17,10 @@
 LANES = 128
 KT = 256
 SLAB = 128
-SLABS = 10
+SLABS = 12
+EARLY = 2
 SEQ_BLOCK = 16
+PROJECT_VMEM = 36 << 20
 
 
 def shift_down(bits, places):
@@ -37,11 +39,30 @@
     return jnp.where(top < 0, -2.0, 0.0).astype(jnp.bfloat16)
 
 
-def grad_kernel(lens_ref, up_any, outg_any, hid_any, out_ref, up_ref, outg_ref, hid_ref, sems):
+def grad_kernel(
+    lens_ref,
+    seeds_ref,
+    grp_ref,
+    up_any,
+    outg_any,
+    hid_any,
+    out_ref,
+    held_any,
+    up_ref,
+    outg_ref,
+    hid_ref,
+    pos_ref,
+    turn_ref,
+    held_ref,
+    sems,
+    held_sems,
+):
     seq = pl.program_id(0)
     blocks, toks, outs = outg_ref.shape
     width = hid_ref.shape[2]
     groups, wide, _, rows, cols = out_ref.shape
+    chunk = held_ref.shape[2]
+    first_row = grp_ref[0] * rows
 
     def loads(blk):
         return (
@@ -56,6 +77,20 @@
         load_outg.start()
     for _, _, load_hid in copies:
         load_hid.start()
+
+    def hold(slab):
+        @pl.when(seq == 0)
+        def _():
+            for pair, word in slab_pairs(pos_ref, seeds_ref, turn_ref, first_row, slab, rows, cols // chunk, chunk):
+                held_ref[slab, pair] = word
+            pltpu.make_async_copy(held_ref.at[slab], held_any.at[slab], held_sems.at[slab]).start()
+
+    @pl.when(seq == 0)
+    def _():
+        fill_positions(pos_ref)
+        fill_turns(turn_ref, seeds_ref, first_row, rows)
+
+    hold(0)
     low = jnp.zeros((toks, up_ref.shape[1]), jnp.float32)
     for blk, (load_up, load_outg, _) in enumerate(copies):
         load_up.wait()
@@ -66,6 +101,7 @@
     live = lax.broadcasted_iota(jnp.int32, low.shape, 0) < lens_ref[seq]
     low = jnp.where(live, low, 0.0).T.astype(jnp.bfloat16)
     count = lens_ref[seq].astype(jnp.float32)
+    hold(1)
     for blk, (_, _, load_hid) in enumerate(copies):
         load_hid.wait()
         summed = jnp.dot(low, hid_ref[blk], preferred_element_type=jnp.float32)
@@ -76,29 +112,46 @@
                     grp * rows : (grp + 1) * rows, own * cols : (own + 1) * cols
                 ]
 
-
-def seq_grads(hidden, output_gradient, adapter_up_factor, lengths, groups, wide):
+    @pl.when(seq == 0)
+    def _():
+        for slab in range(EARLY):
+            pltpu.make_async_copy(held_ref.at[slab], held_any.at[slab], held_sems.at[slab]).wait()
+
+
+def seq_grads(hidden, output_gradient, adapter_up_factor, lengths, seeds, grp, groups, wide):
     seqs, toks, width = hidden.shape
     outs, rank = adapter_up_factor.shape
     rows, cols = rank // groups, width // wide
+    chunk = min(256, cols)
+    pairs = rows * cols // chunk // 2
     blocks = 4
     return pl.pallas_call(
         grad_kernel,
-        out_shape=jax.ShapeDtypeStruct((groups, wide, seqs, rows, cols), jnp.bfloat16),
+        out_shape=(
+            jax.ShapeDtypeStruct((groups, wide, seqs, rows, cols), jnp.bfloat16),
+            jax.ShapeDtypeStruct((SLABS, pairs, chunk, SLAB), jnp.int32),
+        ),
         grid_spec=pltpu.PrefetchScalarGridSpec(
-            num_scalar_prefetch=1,
+            num_scalar_prefetch=3,
             grid=(seqs,),
             in_specs=[pl.BlockSpec(memory_space=pl.ANY)] * 3,
-            out_specs=pl.BlockSpec((groups, wide, 1, rows, cols), lambda s, n: (0, 0, s, 0, 0)),
+            out_specs=(
+                pl.BlockSpec((groups, wide, 1, rows, cols), lambda s, *_: (0, 0, s, 0, 0)),
+                pl.BlockSpec(memory_space=pl.ANY),
+            ),
             scratch_shapes=[
                 pltpu.VMEM((blocks, rank, outs // blocks), jnp.bfloat16),
                 pltpu.VMEM((blocks, toks, outs // blocks), jnp.bfloat16),
                 pltpu.VMEM((blocks, toks, width // blocks), jnp.bfloat16),
+                pltpu.VMEM((CB, SLAB), jnp.int32),
+                pltpu.SMEM((cols // CB,), jnp.int32),
+                pltpu.VMEM((EARLY, pairs, chunk, SLAB), jnp.int32),
                 pltpu.SemaphoreType.DMA((3, blocks)),
+                pltpu.SemaphoreType.DMA((EARLY,)),
             ],
         ),
         name="seq_grads",
-    )(lengths, adapter_up_factor.T, output_gradient, hidden)
+    )(lengths, seeds, grp, adapter_up_factor.T, output_gradient, hidden)
 
 
 def fill_positions(pos_ref):
@@ -120,11 +173,22 @@
 
 
 def slot_row(turn, slot, rows):
+    if rows & (rows - 1) == 0:
+        return (turn + slot) & (rows - 1)
     return lax.rem(turn + slot, jnp.int32(rows))
 
 
 def slot_wraps(slot, rows):
     return slot >= rows - 2 or rows * BLOCK + SPAN > 2**31
+
+
+def slab_pairs(pos_ref, seeds_ref, turn_ref, first_row, slab, rows, halves, chunk):
+    def top_of(entry):
+        slot, half = divmod(entry, halves)
+        return slot_tile(pos_ref, seeds_ref, turn_ref, first_row, slab * SLAB, slot, half, chunk // CB, rows)
+
+    for pair in range(rows * halves // 2):
+        yield pair, top_of(2 * pair) | shift_down(top_of(2 * pair + 1), 17)
 
 
 def slot_tile(pos_ref, seeds_ref, turn_ref, first_row, feat, slot, half, parts, rows):
@@ -135,25 +199,21 @@
     return mixed(jnp.concatenate(tile, axis=0) if parts > 1 else tile[0], slot_wraps(slot, rows))
 
 
-def presign_kernel(seeds_ref, grp_ref, out_ref, pos_ref, turn_ref, *, rows, halves):
+def presign_kernel(seeds_ref, grp_ref, early_ref, out_ref, pos_ref, turn_ref, *, rows, halves):
     slab = pl.program_id(0)
     first_row = grp_ref[0] * rows
-    pairs, chunk, feats = out_ref.shape[1:]
+    chunk = out_ref.shape[2]
 
     @pl.when(slab == 0)
     def _():
         fill_positions(pos_ref)
         fill_turns(turn_ref, seeds_ref, first_row, rows)
 
-    def top_of(entry):
-        slot, half = divmod(entry, halves)
-        return slot_tile(pos_ref, seeds_ref, turn_ref, first_row, slab * feats, slot, half, chunk // CB, rows)
-
-    for pair in range(pairs):
-        out_ref[0, pair] = top_of(2 * pair) | shift_down(top_of(2 * pair + 1), 17)
-
-
-def presign(seeds, grp, rows, cols):
+    for pair, word in slab_pairs(pos_ref, seeds_ref, turn_ref, first_row, EARLY + slab, rows, halves, chunk):
+        out_ref[0, pair] = word
+
+
+def presign(seeds, grp, held, rows, cols):
     chunk = min(256, cols)
     chunks = rows * cols // chunk
     return pl.pallas_call(
@@ -161,15 +221,17 @@
         out_shape=jax.ShapeDtypeStruct((SLABS, chunks // 2, chunk, SLAB), jnp.int32),
         grid_spec=pltpu.PrefetchScalarGridSpec(
             num_scalar_prefetch=2,
-            grid=(SLABS,),
-            out_specs=pl.BlockSpec((1, chunks // 2, chunk, SLAB), lambda i, s, g: (i, 0, 0, 0)),
+            grid=(SLABS - EARLY,),
+            in_specs=[pl.BlockSpec(memory_space=pl.ANY)],
+            out_specs=pl.BlockSpec((1, chunks // 2, chunk, SLAB), lambda i, s, g: (EARLY + i, 0, 0, 0)),
             scratch_shapes=[pltpu.VMEM((CB, SLAB), jnp.int32), pltpu.SMEM((cols // CB,), jnp.int32)],
         ),
         cost_estimate=pl.CostEstimate(
             flops=SLABS * SLAB * rows * cols * 10, bytes_accessed=SLABS * SLAB * rows * cols * 2, transcendentals=0
         ),
+        input_output_aliases={2: 0},
         name="presign",
-    )(seeds, grp)
+    )(seeds, grp, held)
 
 
 def project_kernel(
@@ -179,7 +241,9 @@
     first_ref,
     second_ref,
     held_ref,
+    last_ref,
     out_ref,
+    feat_ref,
     wide_ref,
     upd_ref,
     sum_ref,
@@ -228,31 +292,36 @@
                 total += upd.astype(jnp.float32)
         sum_ref[...] = jnp.broadcast_to(jnp.sum(total, axis=1, keepdims=True), sum_ref.shape)
 
-    feats = out_ref.shape[0] // seqs
+    feats = feat_ref.shape[0] // seqs
     held_feats = SLABS * SLAB
     start = jnp.broadcast_to(sum_ref[:, :1], (seqs, KT))
 
     def put(first_feat, acc):
         for part in range(acc.shape[1] // LANES):
-            out_ref[pl.ds(first_feat // LANES + part, seqs, stride=feats), :] = acc[:, part * LANES : (part + 1) * LANES]
-
-    def tile_step(with_held):
+            feat_ref[pl.ds(first_feat // LANES + part, seqs, stride=feats), :] = acc[:, part * LANES : (part + 1) * LANES]
+
+    def tile_step(slabs):
         feat = held_feats + step * KT
-        acc, held_acc = start, start[:, :SLAB]
+        accs = [start] + [start[:, :SLAB]] * len(slabs)
         for entry in range(upd_ref.shape[0]):
             slot, half = divmod(entry, halves)
-            weights = sign_weights(slot_tile(pos_ref, seeds_ref, turn_ref, first_row, feat, slot, half, parts, rows))
-            acc += jnp.dot(upd_ref[entry], weights, preferred_element_type=jnp.float32)
-            if with_held:
-                top = held_ref[0, entry // 2]
-                weights = sign_weights(top << 17 if entry % 2 else top)
-                held_acc += jnp.dot(upd_ref[entry], weights, preferred_element_type=jnp.float32)
-        put(feat, acc)
-        if with_held:
-            put(step * SLAB, held_acc)
-
-    pl.when(step < SLABS)(lambda: tile_step(True))
-    pl.when(step >= SLABS)(lambda: tile_step(False))
+            tops = [slot_tile(pos_ref, seeds_ref, turn_ref, first_row, feat, slot, half, parts, rows)]
+            words = [ref[0, entry // 2] for ref, _ in slabs]
+            tops += [word << 17 if entry % 2 else word for word in words]
+            for pos, top in enumerate(tops):
+                accs[pos] += jnp.dot(upd_ref[entry], sign_weights(top), preferred_element_type=jnp.float32)
+        put(feat, accs[0])
+        for (_, slab), acc in zip(slabs, accs[1:]):
+            put(slab * SLAB, acc)
+
+    steps = pl.num_programs(0)
+    twice = SLABS - steps
+    pl.when(step < steps - twice)(lambda: tile_step([(held_ref, step)]))
+    pl.when(step >= steps - twice)(lambda: tile_step([(held_ref, step), (last_ref, step + twice)]))
+
+    @pl.when(step == steps - 1)
+    def _():
+        out_ref[...] = feat_ref[...].astype(out_ref.dtype)
 
 
 def project(grads, first, second, seeds, grp, held):
@@ -260,20 +329,26 @@
     chunk = min(256, cols)
     chunks = rows * cols // chunk
     feats = K // LANES
+    steps = (K - SLABS * SLAB) // KT
     return pl.pallas_call(
         project_kernel,
-        out_shape=jax.ShapeDtypeStruct((seqs * feats, LANES), jnp.float32),
+        out_shape=jax.ShapeDtypeStruct((seqs * feats, LANES), jnp.bfloat16),
         grid_spec=pltpu.PrefetchScalarGridSpec(
             num_scalar_prefetch=2,
-            grid=((K - SLABS * SLAB) // KT,),
+            grid=(steps,),
             in_specs=[
                 pl.BlockSpec(memory_space=pltpu.VMEM),
                 pl.BlockSpec((rows, cols), lambda i, s, g: (g[0], 0)),
                 pl.BlockSpec((rows, cols), lambda i, s, g: (g[0], 0)),
-                pl.BlockSpec((1, chunks // 2, chunk, SLAB), lambda i, s, g: (jnp.minimum(i, SLABS - 1), 0, 0, 0)),
+                pl.BlockSpec((1, chunks // 2, chunk, SLAB), lambda i, s, g: (i, 0, 0, 0)),
+                pl.BlockSpec(
+                    (1, chunks // 2, chunk, SLAB),
+                    lambda i, s, g: (jnp.maximum(i + SLABS - steps, steps), 0, 0, 0),
+                ),
             ],
             out_specs=pl.BlockSpec((seqs * feats, LANES), lambda i, s, g: (0, 0)),
             scratch_shapes=[
+                pltpu.VMEM((seqs * feats, LANES), jnp.float32),
                 pltpu.VMEM((pl.cdiv(cols, LANES), rows, seqs, LANES), jnp.bfloat16),
                 pltpu.VMEM((chunks, seqs, chunk), jnp.bfloat16),
                 pltpu.VMEM((seqs, LANES), jnp.float32),
@@ -281,8 +356,15 @@
                 pltpu.SMEM((cols // CB,), jnp.int32),
             ],
         ),
+        compiler_params=pltpu.CompilerParams(vmem_limit_bytes=PROJECT_VMEM),
         name="project",
-    )(seeds, grp, grads, first, second, held)
+    )(seeds, grp, grads, first, second, held, held)
+
+
+def finish_kernel(partial_ref, out_ref):
+    total = jnp.sum(partial_ref[...].astype(jnp.float32), axis=0)
+    mean = jnp.sum(total * total, axis=(1, 2), keepdims=True) / K
+    out_ref[...] = total * lax.rsqrt(mean + 1e-06)
 
 
 def shards(
@@ -297,18 +379,22 @@
     groups, wide = lax.axis_size("grp"), lax.axis_size("wide")
     devices = groups * wide
     own_seqs = hidden.shape[0]
-    grads = seq_grads(hidden, output_gradient, adapter_up_factor, lengths, groups, wide)
+    grp = lax.axis_index("grp").astype(jnp.int32).reshape(1)
+    grads, held = seq_grads(hidden, output_gradient, adapter_up_factor, lengths, seeds, grp, groups, wide)
     rows, cols = grads.shape[-2:]
-    grp = lax.axis_index("grp").astype(jnp.int32).reshape(1)
     grads = grads.reshape(devices, own_seqs, rows, cols)
-    held = presign(seeds, grp, rows, cols)
+    held = presign(seeds, grp, held, rows, cols)
     grads = lax.all_to_all(grads, AXES, 0, 0, tiled=True).reshape(devices * own_seqs, rows, cols)
+    grads = pltpu.with_memory_space_constraint(grads, pltpu.VMEM)
     partial = project(grads, first_moment_estimate, second_moment_estimate, seeds, grp, held)
     partial = partial.reshape(devices, own_seqs, K // LANES, LANES)
     partial = lax.all_to_all(partial, AXES, 0, 0, tiled=True)
-    own_rows = jnp.sum(partial, axis=0)
-    scale = lax.rsqrt(jnp.mean(own_rows * own_rows, axis=(1, 2), keepdims=True) + 1e-06)
-    return (own_rows * scale).reshape(own_seqs, K)
+    out = pl.pallas_call(
+        finish_kernel,
+        out_shape=jax.ShapeDtypeStruct((own_seqs, K // LANES, LANES), jnp.float32),
+        name="finish",
+    )(partial)
+    return out.reshape(own_seqs, K)
 
 
 def solution(mesh):

time: 136 us -> 130 us (0.956)
  blocking collectives: 21.7 us -> 16 us
  Pallas kernels: 103 us -> 106 us
    pallas_call x1 -> x2, Pallas kernels: 6.48 us -> 12.8 us  [the longest x1 11.1 us: seq_grads(): pl.pallas_call(grad_kernel, out_shape=(jax.ShapeDtypeStruct((groups, wide...]
    all_to_all x1, blocking collectives: 21.7 us -> 16 us  [shards(): partial = lax.all_to_all(partial, AXES, 0, 0, tiled=True)]
    pallas_call x1, Pallas kernels: 68.5 us -> 65.4 us  [project(): pl.pallas_call(project_kernel, out_shape=jax.ShapeDtypeStruct((seqs * fea...]
  transfers between devices with their start and end apart: 1 -> 1, of which waited for: 0 -> 0; matrix products, arithmetic and copies ran while one was open for 0% -> 0% of each run, Pallas kernels for 20% -> 21%
where the time goes in v4:
time: 130 us
  Pallas kernels  106 us (82%)
  blocking collectives  16 us (12%)
  starting transfers between devices  7.34 us (6%)
    pallas_call x1, Pallas kernels, project(): pl.pallas_call(project_kernel, out_shape=jax.ShapeDtypeStruct((seqs * fea...  65.4 us
    pallas_call x1, Pallas kernels, presign(): pl.pallas_call(functools.partial(presign_kernel, rows=rows, halves=cols /...  27.8 us
    all_to_all x1, blocking collectives, shards(): partial = lax.all_to_all(partial, AXES, 0, 0, tiled=True)  16 us
    pallas_call x1, Pallas kernels, seq_grads(): pl.pallas_call(grad_kernel, out_shape=(jax.ShapeDtypeStruct((groups, wide...  11.1 us
    all_to_all x1, starting transfers between devices, shards(): lax.all_to_all(grads, AXES, 0, 0, tiled=True)  7.34 us
  transfers between devices with their start and end apart: 1, of which 0 were waited for; matrix products, arithmetic and copies ran while one was open for 0% of the time, Pallas kernels for 21%

profile of v4, /device:TPU:0, one launch (start us, length us, event | category | flops | bytes accessed | tf_op | source)
XLA Modules:
  0.0 130.1 jit_solution(2633588934978447307)
XLA Ops:
  0.7 11.1 %seq_grads.1 = (bf16[2,16,1,32,512]{4,3,2,1,0:T(8,128)(2,1)}, s32[12,32,256,128]{3,2,1,0:T(8,128)}) custom-call(s32[1]{0:T(128)S(6)} %copy.11.lens_ref, s32[8]{0:T(128)} %seeds_ref.5, s32[1]{0:T(128)} %bitcast.grp_ref, bf16[64,8192]{1,0:T(8,128)(2,1)} %bitcast.10, bf16[1,256,8192]{2,1,0:T(8,128)(2,1)} %outg_any.1, bf16[1,256,8192]{2,1,0:T(8,128)(2,1)} %hid_any.1), custom_call_target="tpu_custom_call" | custom-call | tf_op jit(solution)/shard_map/seq_grads/pallas_call | solution.py:128
  11.8 7.3 %all-to-all-start = ((bf16[32,1,32,512]{3,2,1,0:T(8,128)(2,1)}), bf16[32,1,32,512]{3,2,1,0:T(8,128)(2,1)S(1)}, u32[]{:S(2)}, u32[]{:S(2)}) async-start(bf16[32,1,32,512]{3,2,1,0:T(8,128)(2,1)} %bitcast.11), calls=%async_computation | async-start | bytes 2097152 | tf_op jit(solution)/shard_map/all_to_all | solution.py:387
  19.1 0.0 copy-start
  19.1 0.0 copy-start.1
  19.2 0.0 copy-start.2
  19.2 27.8 %presign.1.held_ref.last_ref = s32[12,32,256,128]{3,2,1,0:T(8,128)} custom-call(s32[8]{0:T(128)} %seeds_ref.5, s32[1]{0:T(128)} %bitcast.grp_ref, s32[12,32,256,128]{3,2,1,0:T(8,128)} %get-tuple-element.8.early_ref), custom_call_target="tpu_custom_call", output_to_operand_aliasing={{}: (2, {})} | custom-call | flops 251658240 | bytes 50331648 | tf_op jit(solution)/shard_map/presign/pallas_call | solution.py:219
  47.0 0.0 all-to-all-done
  47.0 0.0 copy-done
  47.0 0.0 copy-done.1
  47.0 0.0 copy-done.2
  47.0 65.4 %project.1 = bf16[1024,128]{1,0:T(8,128)(2,1)S(1)} custom-call(s32[8]{0:T(128)S(1)} %copy-done.2, s32[1]{0:T(128)} %bitcast.grp_ref, bf16[32,32,512]{2,1,0:T(8,128)(2,1)S(1)} %bitcast.8, f32[64,512]{1,0:T(8,128)S(1)} %copy-done, f32[64,512]{1,0:T(8,128)S(1)} %copy-done.1, s32[12,32,256,128]{3,2,1,0:T(8,128)} %presign.1.held_ref.last_ref, ...), custom_call_target="tpu_custom_call" | custom-call | tf_op jit(solution)/shard_map/project/pallas_call | solution.py:333
  112.5 16.0 %all_to_all.10.partial_ref = bf16[32,1,32,128]{3,2,1,0:T(8,128)(2,1)} all-to-all(bf16[32,1,32,128]{3,2,1,0:T(8,128)(2,1)S(1)} %bitcast.9), channel_id=1, replica_groups=mesh['grp'=2,'wide'=16] {'grp','wide'}, dimensions={0} | all-to-all | bytes 524288 | tf_op jit(solution)/shard_map/all_to_all | solution.py:391
  128.5 1.7 %finish.1 = f32[1,32,128]{2,1,0:T(8,128)} custom-call(bf16[32,1,32,128]{3,2,1,0:T(8,128)(2,1)} %all_to_all.10.partial_ref), custom_call_target="tpu_custom_call" | custom-call | tf_op jit(solution)/shard_map/finish/pallas_call | solution.py:392
Async XLA Ops:
  11.8 35.2 %all-to-all-start = ((bf16[32,1,32,512]{3,2,1,0:T(8,128)(2,1)}), bf16[32,1,32,512]{3,2,1,0:T(8,128)(2,1)S(1)}, u32[]{:S(2)}, u32[]{:S(2)}) async-start(bf16[32,1,32,512]{3,2,1,0:T(8,128)(2,1)} %bitcast.11), calls=%async_computation | async-start | bytes 2097152 | tf_op jit(solution)/shard_map/all_to_all | solution.py:387
  19.1 27.9 %copy-start = (f32[64,512]{1,0:T(8,128)S(1)}, f32[64,512]{1,0:T(8,128)}, u32[]{:S(2)}) copy-start(f32[64,512]{1,0:T(8,128)} %first_ref.1) | copy-start | bytes 393220
  19.1 27.8 %copy-start.1 = (f32[64,512]{1,0:T(8,128)S(1)}, f32[64,512]{1,0:T(8,128)}, u32[]{:S(2)}) copy-start(f32[64,512]{1,0:T(8,128)} %second_ref.1) | copy-start | bytes 393220
  19.2 27.8 %copy-start.2 = (s32[8]{0:T(128)S(1)}, s32[8]{0:T(128)}, u32[]{:S(2)}) copy-start(s32[8]{0:T(128)} %seeds_ref.5) | copy-start | bytes 100

commit v5 on v4

--- a/solution.py
+++ b/solution.py
@@ -56,6 +56,8 @@
     held_ref,
     sems,
     held_sems,
+    *,
+    single,
 ):
     seq = pl.program_id(0)
     blocks, toks, outs = outg_ref.shape
@@ -78,19 +80,35 @@
     for _, _, load_hid in copies:
         load_hid.start()
 
-    def hold(slab):
-        @pl.when(seq == 0)
-        def _():
-            for pair, word in slab_pairs(pos_ref, seeds_ref, turn_ref, first_row, slab, rows, cols // chunk, chunk):
+    pieces = held_ref.shape[1] // blocks
+
+    def held_copy(slab, blk):
+        span = pl.ds(blk * pieces, pieces)
+        return pltpu.make_async_copy(held_ref.at[slab, span], held_any.at[slab, span], held_sems.at[slab, blk])
+
+    def hold(slab, blk):
+        def fill():
+            span = range(blk * pieces, (blk + 1) * pieces)
+            for pair, word in slab_pairs(pos_ref, seeds_ref, turn_ref, first_row, slab, rows, cols // chunk, chunk, span):
                 held_ref[slab, pair] = word
-            pltpu.make_async_copy(held_ref.at[slab], held_any.at[slab], held_sems.at[slab]).start()
-
-    @pl.when(seq == 0)
-    def _():
+            held_copy(slab, blk).start()
+
+        once(fill)
+
+    def once(task):
+        if single:
+            task()
+        else:
+            pl.when(seq == 0)(task)
+
+    def start_hold():
         fill_positions(pos_ref)
         fill_turns(turn_ref, seeds_ref, first_row, rows)
 
-    hold(0)
+    once(start_hold)
+    for slab in range(EARLY):
+        for blk in range(blocks):
+            hold(slab, blk)
     low = jnp.zeros((toks, up_ref.shape[1]), jnp.float32)
     for blk, (load_up, load_outg, _) in enumerate(copies):
         load_up.wait()
@@ -101,7 +119,6 @@
     live = lax.broadcasted_iota(jnp.int32, low.shape, 0) < lens_ref[seq]
     low = jnp.where(live, low, 0.0).T.astype(jnp.bfloat16)
     count = lens_ref[seq].astype(jnp.float32)
-    hold(1)
     for blk, (_, _, load_hid) in enumerate(copies):
         load_hid.wait()
         summed = jnp.dot(low, hid_ref[blk], preferred_element_type=jnp.float32)
@@ -112,10 +129,12 @@
                     grp * rows : (grp + 1) * rows, own * cols : (own + 1) * cols
                 ]
 
-    @pl.when(seq == 0)
-    def _():
+    def end_hold():
         for slab in range(EARLY):
-            pltpu.make_async_copy(held_ref.at[slab], held_any.at[slab], held_sems.at[slab]).wait()
+            for blk in range(blocks):
+                held_copy(slab, blk).wait()
+
+    once(end_hold)
 
 
 def seq_grads(hidden, output_gradient, adapter_up_factor, lengths, seeds, grp, groups, wide):
@@ -126,7 +145,7 @@
     pairs = rows * cols // chunk // 2
     blocks = 4
     return pl.pallas_call(
-        grad_kernel,
+        functools.partial(grad_kernel, single=seqs == 1),
         out_shape=(
             jax.ShapeDtypeStruct((groups, wide, seqs, rows, cols), jnp.bfloat16),
             jax.ShapeDtypeStruct((SLABS, pairs, chunk, SLAB), jnp.int32),
@@ -147,7 +166,7 @@
                 pltpu.SMEM((cols // CB,), jnp.int32),
                 pltpu.VMEM((EARLY, pairs, chunk, SLAB), jnp.int32),
                 pltpu.SemaphoreType.DMA((3, blocks)),
-                pltpu.SemaphoreType.DMA((EARLY,)),
+                pltpu.SemaphoreType.DMA((EARLY, blocks)),
             ],
         ),
         name="seq_grads",
@@ -182,12 +201,12 @@
     return slot >= rows - 2 or rows * BLOCK + SPAN > 2**31
 
 
-def slab_pairs(pos_ref, seeds_ref, turn_ref, first_row, slab, rows, halves, chunk):
+def slab_pairs(pos_ref, seeds_ref, turn_ref, first_row, slab, rows, halves, chunk, pairs):
     def top_of(entry):
         slot, half = divmod(entry, halves)
         return slot_tile(pos_ref, seeds_ref, turn_ref, first_row, slab * SLAB, slot, half, chunk // CB, rows)
 
-    for pair in range(rows * halves // 2):
+    for pair in pairs:
         yield pair, top_of(2 * pair) | shift_down(top_of(2 * pair + 1), 17)
 
 
@@ -202,14 +221,14 @@
 def presign_kernel(seeds_ref, grp_ref, early_ref, out_ref, pos_ref, turn_ref, *, rows, halves):
     slab = pl.program_id(0)
     first_row = grp_ref[0] * rows
-    chunk = out_ref.shape[2]
+    pairs, chunk = range(out_ref.shape[1]), out_ref.shape[2]
 
     @pl.when(slab == 0)
     def _():
         fill_positions(pos_ref)
         fill_turns(turn_ref, seeds_ref, first_row, rows)
 
-    for pair, word in slab_pairs(pos_ref, seeds_ref, turn_ref, first_row, EARLY + slab, rows, halves, chunk):
+    for pair, word in slab_pairs(pos_ref, seeds_ref, turn_ref, first_row, EARLY + slab, rows, halves, chunk, pairs):
         out_ref[0, pair] = word
 
 
@@ -240,8 +259,7 @@
     grad_ref,
     first_ref,
     second_ref,
-    held_ref,
-    last_ref,
+    held_any,
     out_ref,
     feat_ref,
     wide_ref,
@@ -249,16 +267,27 @@
     sum_ref,
     pos_ref,
     turn_ref,
+    held_ref,
+    held_sems,
 ):
     step = pl.program_id(0)
+    steps = pl.num_programs(0)
+    twice = SLABS - steps
     seqs, rows, cols = grad_ref.shape
     chunk = upd_ref.shape[2]
     halves = cols // chunk
     parts = chunk // CB
     first_row = grp_ref[0] * rows
 
+    def held_copy(slab, spot):
+        return pltpu.make_async_copy(held_any.at[slab], held_ref.at[spot], held_sems.at[spot])
+
     @pl.when(step == 0)
     def _():
+        for spot in range(2):
+            held_copy(spot, spot).start()
+        for pos in range(twice):
+            held_copy(steps + pos, 2 + pos).start()
         fill_positions(pos_ref)
         fill_turns(turn_ref, seeds_ref, first_row, rows)
         width = min(LANES, cols)
@@ -303,21 +332,26 @@
     def tile_step(slabs):
         feat = held_feats + step * KT
         accs = [start] + [start[:, :SLAB]] * len(slabs)
+        for slab, spot in slabs:
+            held_copy(slab, spot).wait()
         for entry in range(upd_ref.shape[0]):
             slot, half = divmod(entry, halves)
             tops = [slot_tile(pos_ref, seeds_ref, turn_ref, first_row, feat, slot, half, parts, rows)]
-            words = [ref[0, entry // 2] for ref, _ in slabs]
+            words = [held_ref[spot, entry // 2] for _, spot in slabs]
             tops += [word << 17 if entry % 2 else word for word in words]
             for pos, top in enumerate(tops):
                 accs[pos] += jnp.dot(upd_ref[entry], sign_weights(top), preferred_element_type=jnp.float32)
         put(feat, accs[0])
-        for (_, slab), acc in zip(slabs, accs[1:]):
+        for (slab, _), acc in zip(slabs, accs[1:]):
             put(slab * SLAB, acc)
 
-    steps = pl.num_programs(0)
-    twice = SLABS - steps
-    pl.when(step < steps - twice)(lambda: tile_step([(held_ref, step)]))
-    pl.when(step >= steps - twice)(lambda: tile_step([(held_ref, step), (last_ref, step + twice)]))
+    spot = lax.rem(step, 2)
+    pl.when(step < steps - twice)(lambda: tile_step([(step, spot)]))
+    pl.when(step >= steps - twice)(lambda: tile_step([(step, spot), (step + twice, step - (steps - twice) + 2)]))
+
+    @pl.when(step + 2 < steps)
+    def _():
+        held_copy(step + 2, spot).start()
 
     @pl.when(step == steps - 1)
     def _():
@@ -340,11 +374,7 @@
                 pl.BlockSpec(memory_space=pltpu.VMEM),
                 pl.BlockSpec((rows, cols), lambda i, s, g: (g[0], 0)),
                 pl.BlockSpec((rows, cols), lambda i, s, g: (g[0], 0)),
-                pl.BlockSpec((1, chunks // 2, chunk, SLAB), lambda i, s, g: (i, 0, 0, 0)),
-                pl.BlockSpec(
-                    (1, chunks // 2, chunk, SLAB),
-                    lambda i, s, g: (jnp.maximum(i + SLABS - steps, steps), 0, 0, 0),
-                ),
+                pl.BlockSpec(memory_space=pl.ANY),
             ],
             out_specs=pl.BlockSpec((seqs * feats, LANES), lambda i, s, g: (0, 0)),
             scratch_shapes=[
@@ -354,11 +384,13 @@
                 pltpu.VMEM((seqs, LANES), jnp.float32),
                 pltpu.VMEM((CB, KT), jnp.int32),
                 pltpu.SMEM((cols // CB,), jnp.int32),
+                pltpu.VMEM((2 + SLABS - steps, chunks // 2, chunk, SLAB), jnp.int32),
+                pltpu.SemaphoreType.DMA((2 + SLABS - steps,)),
             ],
         ),
         compiler_params=pltpu.CompilerParams(vmem_limit_bytes=PROJECT_VMEM),
         name="project",
-    )(seeds, grp, grads, first, second, held, held)
+    )(seeds, grp, grads, first, second, held)
 
 
 def finish_kernel(partial_ref, out_ref):

time: 130 us -> 126 us (0.969)
  Pallas kernels: 106 us -> 101 us
    pallas_call x1, Pallas kernels: 65.4 us -> 61.2 us  [project(): pl.pallas_call(project_kernel, out_shape=jax.ShapeDtypeStruct((seqs * fea...]
  transfers between devices with their start and end apart: 1 -> 1, of which waited for: 0 -> 0; matrix products, arithmetic and copies ran while one was open for 0% -> 0% of each run, Pallas kernels for 21% -> 22%
where the time goes in v5:
time: 126 us; the launch traced here: 125 us
  Pallas kernels  101 us (80%)
  blocking collectives  16 us (13%)
  starting transfers between devices  7.34 us (6%)
    pallas_call x1, Pallas kernels, project(): pl.pallas_call(project_kernel, out_shape=jax.ShapeDtypeStruct((seqs * fea...  61.2 us
    pallas_call x1, Pallas kernels, presign(): pl.pallas_call(functools.partial(presign_kernel, rows=rows, halves=cols /...  27.8 us
    all_to_all x1, blocking collectives, shards(): partial = lax.all_to_all(partial, AXES, 0, 0, tiled=True)  16 us
    pallas_call x1, Pallas kernels, seq_grads(): pl.pallas_call(functools.partial(grad_kernel, single=seqs == 1), out_shap...  10.7 us
    all_to_all x1, starting transfers between devices, shards(): lax.all_to_all(grads, AXES, 0, 0, tiled=True)  7.34 us
  transfers between devices with their start and end apart: 1, of which 0 were waited for; matrix products, arithmetic and copies ran while one was open for 0% of the time, Pallas kernels for 22%

profile of v5, /device:TPU:0, one launch (start us, length us, event | category | flops | bytes accessed | tf_op | source)
XLA Modules:
  0.0 125.5 jit_solution(17619618410134993359)
XLA Ops:
  0.7 10.7 %seq_grads.1 = (bf16[2,16,1,32,512]{4,3,2,1,0:T(8,128)(2,1)}, s32[12,32,256,128]{3,2,1,0:T(8,128)}) custom-call(s32[1]{0:T(128)S(6)} %copy.11.lens_ref, s32[8]{0:T(128)} %seeds_ref.5, s32[1]{0:T(128)} %bitcast.grp_ref, bf16[64,8192]{1,0:T(8,128)(2,1)} %bitcast.10, bf16[1,256,8192]{2,1,0:T(8,128)(2,1)} %outg_any.1, bf16[1,256,8192]{2,1,0:T(8,128)(2,1)} %hid_any.1), custom_call_target="tpu_custom_call" | custom-call | tf_op jit(solution)/shard_map/seq_grads/pallas_call | solution.py:147
  11.3 7.3 %all-to-all-start = ((bf16[32,1,32,512]{3,2,1,0:T(8,128)(2,1)}), bf16[32,1,32,512]{3,2,1,0:T(8,128)(2,1)S(1)}, u32[]{:S(2)}, u32[]{:S(2)}) async-start(bf16[32,1,32,512]{3,2,1,0:T(8,128)(2,1)} %bitcast.11), calls=%async_computation | async-start | bytes 2097152 | tf_op jit(solution)/shard_map/all_to_all | solution.py:419
  18.7 0.0 copy-start
  18.7 0.0 copy-start.1
  18.7 0.0 copy-start.2
  18.7 27.8 %presign.1.held_any = s32[12,32,256,128]{3,2,1,0:T(8,128)} custom-call(s32[8]{0:T(128)} %seeds_ref.5, s32[1]{0:T(128)} %bitcast.grp_ref, s32[12,32,256,128]{3,2,1,0:T(8,128)} %get-tuple-element.8.early_ref), custom_call_target="tpu_custom_call", output_to_operand_aliasing={{}: (2, {})} | custom-call | flops 251658240 | bytes 50331648 | tf_op jit(solution)/shard_map/presign/pallas_call | solution.py:238
  46.5 0.0 all-to-all-done
  46.5 0.0 copy-done
  46.5 0.0 copy-done.1
  46.5 0.0 copy-done.2
  46.5 61.2 %project.1 = bf16[1024,128]{1,0:T(8,128)(2,1)S(1)} custom-call(s32[8]{0:T(128)S(1)} %copy-done.2, s32[1]{0:T(128)} %bitcast.grp_ref, bf16[32,32,512]{2,1,0:T(8,128)(2,1)S(1)} %bitcast.8, f32[64,512]{1,0:T(8,128)S(1)} %copy-done, f32[64,512]{1,0:T(8,128)S(1)} %copy-done.1, s32[12,32,256,128]{3,2,1,0:T(8,128)} %presign.1.held_any), custom_call_target="tpu_custom_call" | custom-call | tf_op jit(solution)/shard_map/project/pallas_call | solution.py:367
  107.8 16.0 %all_to_all.10.partial_ref = bf16[32,1,32,128]{3,2,1,0:T(8,128)(2,1)} all-to-all(bf16[32,1,32,128]{3,2,1,0:T(8,128)(2,1)S(1)} %bitcast.9), channel_id=1, replica_groups=mesh['grp'=2,'wide'=16] {'grp','wide'}, dimensions={0} | all-to-all | bytes 524288 | tf_op jit(solution)/shard_map/all_to_all | solution.py:423
  123.8 1.7 %finish.1 = f32[1,32,128]{2,1,0:T(8,128)} custom-call(bf16[32,1,32,128]{3,2,1,0:T(8,128)(2,1)} %all_to_all.10.partial_ref), custom_call_target="tpu_custom_call" | custom-call | tf_op jit(solution)/shard_map/finish/pallas_call | solution.py:424
Async XLA Ops:
  11.3 35.2 %all-to-all-start = ((bf16[32,1,32,512]{3,2,1,0:T(8,128)(2,1)}), bf16[32,1,32,512]{3,2,1,0:T(8,128)(2,1)S(1)}, u32[]{:S(2)}, u32[]{:S(2)}) async-start(bf16[32,1,32,512]{3,2,1,0:T(8,128)(2,1)} %bitcast.11), calls=%async_computation | async-start | bytes 2097152 | tf_op jit(solution)/shard_map/all_to_all | solution.py:419
  18.7 27.9 %copy-start = (f32[64,512]{1,0:T(8,128)S(1)}, f32[64,512]{1,0:T(8,128)}, u32[]{:S(2)}) copy-start(f32[64,512]{1,0:T(8,128)} %first_ref.1) | copy-start | bytes 393220
  18.7 27.8 %copy-start.1 = (f32[64,512]{1,0:T(8,128)S(1)}, f32[64,512]{1,0:T(8,128)}, u32[]{:S(2)}) copy-start(f32[64,512]{1,0:T(8,128)} %second_ref.1) | copy-start | bytes 393220
  18.7 27.8 %copy-start.2 = (s32[8]{0:T(128)S(1)}, s32[8]{0:T(128)}, u32[]{:S(2)}) copy-start(s32[8]{0:T(128)} %seeds_ref.5) | copy-start | bytes 100

commit v6 on v5

--- a/solution.py
+++ b/solution.py
@@ -21,6 +21,8 @@
 EARLY = 2
 SEQ_BLOCK = 16
 PROJECT_VMEM = 36 << 20
+FINISH_VMEM = 8 << 20
+HALVES = 2
 
 
 def shift_down(bits, places):
@@ -219,17 +221,22 @@
 
 
 def presign_kernel(seeds_ref, grp_ref, early_ref, out_ref, pos_ref, turn_ref, *, rows, halves):
-    slab = pl.program_id(0)
+    slab, side = pl.program_id(0), pl.program_id(1)
     first_row = grp_ref[0] * rows
-    pairs, chunk = range(out_ref.shape[1]), out_ref.shape[2]
-
-    @pl.when(slab == 0)
+    pairs, chunk = out_ref.shape[1:3]
+
+    @pl.when((slab == 0) & (side == 0))
     def _():
         fill_positions(pos_ref)
         fill_turns(turn_ref, seeds_ref, first_row, rows)
 
-    for pair, word in slab_pairs(pos_ref, seeds_ref, turn_ref, first_row, EARLY + slab, rows, halves, chunk, pairs):
-        out_ref[0, pair] = word
+    def fill(first):
+        span = range(first, first + pairs)
+        for pair, word in slab_pairs(pos_ref, seeds_ref, turn_ref, first_row, EARLY + slab, rows, halves, chunk, span):
+            out_ref[0, pair - first] = word
+
+    for pos in range(HALVES):
+        pl.when(side == pos)(functools.partial(fill, pos * pairs))
 
 
 def presign(seeds, grp, held, rows, cols):
@@ -240,9 +247,9 @@
         out_shape=jax.ShapeDtypeStruct((SLABS, chunks // 2, chunk, SLAB), jnp.int32),
         grid_spec=pltpu.PrefetchScalarGridSpec(
             num_scalar_prefetch=2,
-            grid=(SLABS - EARLY,),
+            grid=(SLABS - EARLY, HALVES),
             in_specs=[pl.BlockSpec(memory_space=pl.ANY)],
-            out_specs=pl.BlockSpec((1, chunks // 2, chunk, SLAB), lambda i, s, g: (EARLY + i, 0, 0, 0)),
+            out_specs=pl.BlockSpec((1, chunks // 2 // HALVES, chunk, SLAB), lambda i, j, s, g: (EARLY + i, j, 0, 0)),
             scratch_shapes=[pltpu.VMEM((CB, SLAB), jnp.int32), pltpu.SMEM((cols // CB,), jnp.int32)],
         ),
         cost_estimate=pl.CostEstimate(
@@ -421,9 +428,12 @@
     partial = project(grads, first_moment_estimate, second_moment_estimate, seeds, grp, held)
     partial = partial.reshape(devices, own_seqs, K // LANES, LANES)
     partial = lax.all_to_all(partial, AXES, 0, 0, tiled=True)
+    partial = pltpu.with_memory_space_constraint(partial, pltpu.VMEM)
     out = pl.pallas_call(
         finish_kernel,
         out_shape=jax.ShapeDtypeStruct((own_seqs, K // LANES, LANES), jnp.float32),
+        in_specs=[pl.BlockSpec(memory_space=pltpu.VMEM)],
+        compiler_params=pltpu.CompilerParams(vmem_limit_bytes=FINISH_VMEM),
         name="finish",
     )(partial)
     return out.reshape(own_seqs, K)

time: 126 us -> 125 us (level)
  no operation moved by 1% of the time
where the time goes in v6:
time: 125 us
  Pallas kernels  101 us (81%)
  blocking collectives  15.9 us (13%)
  starting transfers between devices  7.34 us (6%)
    pallas_call x1, Pallas kernels, project(): pl.pallas_call(project_kernel, out_shape=jax.ShapeDtypeStruct((seqs * fea...  61.2 us
    pallas_call x1, Pallas kernels, presign(): pl.pallas_call(functools.partial(presign_kernel, rows=rows, halves=cols /...  27.9 us
    all_to_all x1, blocking collectives, shards(): partial = lax.all_to_all(partial, AXES, 0, 0, tiled=True)  15.9 us
    pallas_call x1, Pallas kernels, seq_grads(): pl.pallas_call(functools.partial(grad_kernel, single=seqs == 1), out_shap...  10.7 us
    all_to_all x1, starting transfers between devices, shards(): lax.all_to_all(grads, AXES, 0, 0, tiled=True)  7.34 us
  transfers between devices with their start and end apart: 1, of which 0 were waited for; matrix products, arithmetic and copies ran while one was open for 0% of the time, Pallas kernels for 22%

profile of v6, /device:TPU:0, one launch (start us, length us, event | category | flops | bytes accessed | tf_op | source)
XLA Modules:
  0.0 124.5 jit_solution(2276026558455297920)
XLA Ops:
  0.7 10.7 %seq_grads.1 = (bf16[2,16,1,32,512]{4,3,2,1,0:T(8,128)(2,1)}, s32[12,32,256,128]{3,2,1,0:T(8,128)}) custom-call(s32[1]{0:T(128)S(6)} %copy.11.lens_ref, s32[8]{0:T(128)} %seeds_ref.5, s32[1]{0:T(128)} %bitcast.grp_ref, bf16[64,8192]{1,0:T(8,128)(2,1)} %bitcast.10, bf16[1,256,8192]{2,1,0:T(8,128)(2,1)} %outg_any.1, bf16[1,256,8192]{2,1,0:T(8,128)(2,1)} %hid_any.1), custom_call_target="tpu_custom_call" | custom-call | tf_op jit(solution)/shard_map/seq_grads/pallas_call | solution.py:149
  11.3 7.3 %all-to-all-start = ((bf16[32,1,32,512]{3,2,1,0:T(8,128)(2,1)}), bf16[32,1,32,512]{3,2,1,0:T(8,128)(2,1)S(1)}, u32[]{:S(2)}, u32[]{:S(2)}) async-start(bf16[32,1,32,512]{3,2,1,0:T(8,128)(2,1)} %bitcast.11), calls=%async_computation | async-start | bytes 2097152 | tf_op jit(solution)/shard_map/all_to_all | solution.py:426
  18.7 0.0 copy-start
  18.7 0.0 copy-start.1
  18.7 0.0 copy-start.2
  18.7 27.9 %presign.1.held_any = s32[12,32,256,128]{3,2,1,0:T(8,128)} custom-call(s32[8]{0:T(128)} %seeds_ref.5, s32[1]{0:T(128)} %bitcast.grp_ref, s32[12,32,256,128]{3,2,1,0:T(8,128)} %get-tuple-element.8.early_ref), custom_call_target="tpu_custom_call", output_to_operand_aliasing={{}: (2, {})} | custom-call | flops 251658240 | bytes 50331648 | tf_op jit(solution)/shard_map/presign/pallas_call | solution.py:245
  46.6 0.0 all-to-all-done
  46.6 0.0 copy-done
  46.6 0.0 copy-done.1
  46.6 0.0 copy-done.2
  46.7 61.2 %project.1 = bf16[1024,128]{1,0:T(8,128)(2,1)S(1)} custom-call(s32[8]{0:T(128)S(1)} %copy-done.2, s32[1]{0:T(128)} %bitcast.grp_ref, bf16[32,32,512]{2,1,0:T(8,128)(2,1)S(1)} %bitcast.8, f32[64,512]{1,0:T(8,128)S(1)} %copy-done, f32[64,512]{1,0:T(8,128)S(1)} %copy-done.1, s32[12,32,256,128]{3,2,1,0:T(8,128)} %presign.1.held_any), custom_call_target="tpu_custom_call" | custom-call | tf_op jit(solution)/shard_map/project/pallas_call | solution.py:374
  107.9 15.9 %all_to_all.10.partial_ref = bf16[32,1,32,128]{3,2,1,0:T(8,128)(2,1)S(1)} all-to-all(bf16[32,1,32,128]{3,2,1,0:T(8,128)(2,1)S(1)} %bitcast.9), channel_id=1, replica_groups=mesh['grp'=2,'wide'=16] {'grp','wide'}, dimensions={0} | all-to-all | bytes 524288 | tf_op jit(solution)/shard_map/all_to_all | solution.py:430
  123.8 0.7 finish.1
Async XLA Ops:
  11.3 35.3 %all-to-all-start = ((bf16[32,1,32,512]{3,2,1,0:T(8,128)(2,1)}), bf16[32,1,32,512]{3,2,1,0:T(8,128)(2,1)S(1)}, u32[]{:S(2)}, u32[]{:S(2)}) async-start(bf16[32,1,32,512]{3,2,1,0:T(8,128)(2,1)} %bitcast.11), calls=%async_computation | async-start | bytes 2097152 | tf_op jit(solution)/shard_map/all_to_all | solution.py:426
  18.7 28.0 %copy-start = (f32[64,512]{1,0:T(8,128)S(1)}, f32[64,512]{1,0:T(8,128)}, u32[]{:S(2)}) copy-start(f32[64,512]{1,0:T(8,128)} %first_ref.1) | copy-start | bytes 393220
  18.7 27.9 %copy-start.1 = (f32[64,512]{1,0:T(8,128)S(1)}, f32[64,512]{1,0:T(8,128)}, u32[]{:S(2)}) copy-start(f32[64,512]{1,0:T(8,128)} %second_ref.1) | copy-start | bytes 393220
  18.7 27.9 %copy-start.2 = (s32[8]{0:T(128)S(1)}, s32[8]{0:T(128)}, u32[]{:S(2)}) copy-start(s32[8]{0:T(128)} %seeds_ref.5) | copy-start | bytes 100

commit v7 on v5

--- a/solution.py
+++ b/solution.py
@@ -20,7 +20,10 @@
 SLABS = 12
 EARLY = 2
 SEQ_BLOCK = 16
-PROJECT_VMEM = 36 << 20
+PROJECT_VMEM = 61 << 20
+FINISH_VMEM = 8 << 20
+FAR = SLABS - EARLY
+QUAD_BITS = (1 << 14) - (1 << 31)
 
 
 def shift_down(bits, places):
@@ -89,8 +92,10 @@
     def hold(slab, blk):
         def fill():
             span = range(blk * pieces, (blk + 1) * pieces)
-            for pair, word in slab_pairs(pos_ref, seeds_ref, turn_ref, first_row, slab, rows, cols // chunk, chunk, span):
-                held_ref[slab, pair] = word
+            halves = cols // chunk
+            quads = slab_words(pos_ref, seeds_ref, turn_ref, first_row, FAR + slab, rows, halves, chunk, span, 4)
+            for quad, word in quads:
+                held_ref[slab, quad] = word
             held_copy(slab, blk).start()
 
         once(fill)
@@ -142,13 +147,13 @@
     outs, rank = adapter_up_factor.shape
     rows, cols = rank // groups, width // wide
     chunk = min(256, cols)
-    pairs = rows * cols // chunk // 2
+    quads = rows * cols // chunk // 4
     blocks = 4
     return pl.pallas_call(
         functools.partial(grad_kernel, single=seqs == 1),
         out_shape=(
             jax.ShapeDtypeStruct((groups, wide, seqs, rows, cols), jnp.bfloat16),
-            jax.ShapeDtypeStruct((SLABS, pairs, chunk, SLAB), jnp.int32),
+            jax.ShapeDtypeStruct((EARLY, quads, chunk, SLAB), jnp.int32),
         ),
         grid_spec=pltpu.PrefetchScalarGridSpec(
             num_scalar_prefetch=3,
@@ -164,7 +169,7 @@
                 pltpu.VMEM((blocks, toks, width // blocks), jnp.bfloat16),
                 pltpu.VMEM((CB, SLAB), jnp.int32),
                 pltpu.SMEM((cols // CB,), jnp.int32),
-                pltpu.VMEM((EARLY, pairs, chunk, SLAB), jnp.int32),
+                pltpu.VMEM((EARLY, quads, chunk, SLAB), jnp.int32),
                 pltpu.SemaphoreType.DMA((3, blocks)),
                 pltpu.SemaphoreType.DMA((EARLY, blocks)),
             ],
@@ -201,13 +206,24 @@
     return slot >= rows - 2 or rows * BLOCK + SPAN > 2**31
 
 
-def slab_pairs(pos_ref, seeds_ref, turn_ref, first_row, slab, rows, halves, chunk, pairs):
+def slab_words(pos_ref, seeds_ref, turn_ref, first_row, slab, rows, halves, chunk, words, per_word):
     def top_of(entry):
         slot, half = divmod(entry, halves)
         return slot_tile(pos_ref, seeds_ref, turn_ref, first_row, slab * SLAB, slot, half, chunk // CB, rows)
 
-    for pair in pairs:
-        yield pair, top_of(2 * pair) | shift_down(top_of(2 * pair + 1), 17)
+    def pair_of(entry):
+        return top_of(entry) | shift_down(top_of(entry + 1), 17)
+
+    for word in words:
+        if per_word == 2:
+            yield word, pair_of(2 * word)
+        else:
+            yield word, (pair_of(4 * word) & QUAD_BITS) | shift_down(pair_of(4 * word + 2) & QUAD_BITS, 1)
+
+
+def entry_top(words, entry, per_word):
+    place = (0, 17, 1, 18)[entry % per_word]
+    return words << place if place else words
 
 
 def slot_tile(pos_ref, seeds_ref, turn_ref, first_row, feat, slot, half, parts, rows):
@@ -218,7 +234,7 @@
     return mixed(jnp.concatenate(tile, axis=0) if parts > 1 else tile[0], slot_wraps(slot, rows))
 
 
-def presign_kernel(seeds_ref, grp_ref, early_ref, out_ref, pos_ref, turn_ref, *, rows, halves):
+def presign_kernel(seeds_ref, grp_ref, out_ref, pos_ref, turn_ref, *, rows, halves):
     slab = pl.program_id(0)
     first_row = grp_ref[0] * rows
     pairs, chunk = range(out_ref.shape[1]), out_ref.shape[2]
@@ -228,29 +244,27 @@
         fill_positions(pos_ref)
         fill_turns(turn_ref, seeds_ref, first_row, rows)
 
-    for pair, word in slab_pairs(pos_ref, seeds_ref, turn_ref, first_row, EARLY + slab, rows, halves, chunk, pairs):
+    for pair, word in slab_words(pos_ref, seeds_ref, turn_ref, first_row, slab, rows, halves, chunk, pairs, 2):
         out_ref[0, pair] = word
 
 
-def presign(seeds, grp, held, rows, cols):
+def presign(seeds, grp, rows, cols):
     chunk = min(256, cols)
     chunks = rows * cols // chunk
     return pl.pallas_call(
         functools.partial(presign_kernel, rows=rows, halves=cols // chunk),
-        out_shape=jax.ShapeDtypeStruct((SLABS, chunks // 2, chunk, SLAB), jnp.int32),
+        out_shape=jax.ShapeDtypeStruct((FAR, chunks // 2, chunk, SLAB), jnp.int32),
         grid_spec=pltpu.PrefetchScalarGridSpec(
             num_scalar_prefetch=2,
-            grid=(SLABS - EARLY,),
-            in_specs=[pl.BlockSpec(memory_space=pl.ANY)],
-            out_specs=pl.BlockSpec((1, chunks // 2, chunk, SLAB), lambda i, s, g: (EARLY + i, 0, 0, 0)),
+            grid=(FAR,),
+            out_specs=pl.BlockSpec((1, chunks // 2, chunk, SLAB), lambda i, s, g: (i, 0, 0, 0)),
             scratch_shapes=[pltpu.VMEM((CB, SLAB), jnp.int32), pltpu.SMEM((cols // CB,), jnp.int32)],
         ),
         cost_estimate=pl.CostEstimate(
-            flops=SLABS * SLAB * rows * cols * 10, bytes_accessed=SLABS * SLAB * rows * cols * 2, transcendentals=0
+            flops=FAR * SLAB * rows * cols * 10, bytes_accessed=FAR * SLAB * rows * cols * 2, transcendentals=0
         ),
-        input_output_aliases={2: 0},
         name="presign",
-    )(seeds, grp, held)
+    )(seeds, grp)
 
 
 def project_kernel(
@@ -260,6 +274,7 @@
     first_ref,
     second_ref,
     held_any,
+    early_any,
     out_ref,
     feat_ref,
     wide_ref,
@@ -268,11 +283,12 @@
     pos_ref,
     turn_ref,
     held_ref,
+    early_ref,
     held_sems,
+    early_sems,
 ):
     step = pl.program_id(0)
     steps = pl.num_programs(0)
-    twice = SLABS - steps
     seqs, rows, cols = grad_ref.shape
     chunk = upd_ref.shape[2]
     halves = cols // chunk
@@ -282,12 +298,15 @@
     def held_copy(slab, spot):
         return pltpu.make_async_copy(held_any.at[slab], held_ref.at[spot], held_sems.at[spot])
 
+    def early_copy(slab):
+        return pltpu.make_async_copy(early_any.at[slab], early_ref.at[slab], early_sems.at[slab])
+
     @pl.when(step == 0)
     def _():
         for spot in range(2):
             held_copy(spot, spot).start()
-        for pos in range(twice):
-            held_copy(steps + pos, 2 + pos).start()
+        for slab in range(EARLY):
+            early_copy(slab).start()
         fill_positions(pos_ref)
         fill_turns(turn_ref, seeds_ref, first_row, rows)
         width = min(LANES, cols)
@@ -329,25 +348,29 @@
         for part in range(acc.shape[1] // LANES):
             feat_ref[pl.ds(first_feat // LANES + part, seqs, stride=feats), :] = acc[:, part * LANES : (part + 1) * LANES]
 
-    def tile_step(slabs):
+    def tile_step(early):
         feat = held_feats + step * KT
-        accs = [start] + [start[:, :SLAB]] * len(slabs)
-        for slab, spot in slabs:
-            held_copy(slab, spot).wait()
+        held_copy(step, spot).wait()
+        accs = [start, start[:, :SLAB]]
+        if early is not None:
+            early_copy(early).wait()
+            accs.append(start[:, :SLAB])
         for entry in range(upd_ref.shape[0]):
             slot, half = divmod(entry, halves)
             tops = [slot_tile(pos_ref, seeds_ref, turn_ref, first_row, feat, slot, half, parts, rows)]
-            words = [held_ref[spot, entry // 2] for _, spot in slabs]
-            tops += [word << 17 if entry % 2 else word for word in words]
+            tops.append(entry_top(held_ref[spot, entry // 2], entry, 2))
+            if early is not None:
+                tops.append(entry_top(early_ref[early, entry // 4], entry, 4))
             for pos, top in enumerate(tops):
                 accs[pos] += jnp.dot(upd_ref[entry], sign_weights(top), preferred_element_type=jnp.float32)
         put(feat, accs[0])
-        for (slab, _), acc in zip(slabs, accs[1:]):
-            put(slab * SLAB, acc)
+        put(step * SLAB, accs[1])
+        if early is not None:
+            put((FAR + early) * SLAB, accs[2])
 
     spot = lax.rem(step, 2)
-    pl.when(step < steps - twice)(lambda: tile_step([(step, spot)]))
-    pl.when(step >= steps - twice)(lambda: tile_step([(step, spot), (step + twice, step - (steps - twice) + 2)]))
+    pl.when(step < steps - EARLY)(lambda: tile_step(None))
+    pl.when(step >= steps - EARLY)(lambda: tile_step(step - (steps - EARLY)))
 
     @pl.when(step + 2 < steps)
     def _():
@@ -358,12 +381,13 @@
         out_ref[...] = feat_ref[...].astype(out_ref.dtype)
 
 
-def project(grads, first, second, seeds, grp, held):
+def project(grads, first, second, seeds, grp, held, early):
     seqs, rows, cols = grads.shape
     chunk = min(256, cols)
     chunks = rows * cols // chunk
     feats = K // LANES
     steps = (K - SLABS * SLAB) // KT
+    assert steps == FAR
     return pl.pallas_call(
         project_kernel,
         out_shape=jax.ShapeDtypeStruct((seqs * feats, LANES), jnp.bfloat16),
@@ -375,6 +399,7 @@
                 pl.BlockSpec((rows, cols), lambda i, s, g: (g[0], 0)),
                 pl.BlockSpec((rows, cols), lambda i, s, g: (g[0], 0)),
                 pl.BlockSpec(memory_space=pl.ANY),
+                pl.BlockSpec(memory_space=pl.ANY),
             ],
             out_specs=pl.BlockSpec((seqs * feats, LANES), lambda i, s, g: (0, 0)),
             scratch_shapes=[
@@ -384,13 +409,15 @@
                 pltpu.VMEM((seqs, LANES), jnp.float32),
                 pltpu.VMEM((CB, KT), jnp.int32),
                 pltpu.SMEM((cols // CB,), jnp.int32),
-                pltpu.VMEM((2 + SLABS - steps, chunks // 2, chunk, SLAB), jnp.int32),
-                pltpu.SemaphoreType.DMA((2 + SLABS - steps,)),
+                pltpu.VMEM((2, chunks // 2, chunk, SLAB), jnp.int32),
+                pltpu.VMEM((EARLY, chunks // 4, chunk, SLAB), jnp.int32),
+                pltpu.SemaphoreType.DMA((2,)),
+                pltpu.SemaphoreType.DMA((EARLY,)),
             ],
         ),
         compiler_params=pltpu.CompilerParams(vmem_limit_bytes=PROJECT_VMEM),
         name="project",
-    )(seeds, grp, grads, first, second, held)
+    )(seeds, grp, grads, first, second, held, early)
 
 
 def finish_kernel(partial_ref, out_ref):
@@ -412,18 +439,21 @@
     devices = groups * wide
     own_seqs = hidden.shape[0]
     grp = lax.axis_index("grp").astype(jnp.int32).reshape(1)
-    grads, held = seq_grads(hidden, output_gradient, adapter_up_factor, lengths, seeds, grp, groups, wide)
+    grads, early = seq_grads(hidden, output_gradient, adapter_up_factor, lengths, seeds, grp, groups, wide)
     rows, cols = grads.shape[-2:]
     grads = grads.reshape(devices, own_seqs, rows, cols)
-    held = presign(seeds, grp, held, rows, cols)
+    held = presign(seeds, grp, rows, cols)
     grads = lax.all_to_all(grads, AXES, 0, 0, tiled=True).reshape(devices * own_seqs, rows, cols)
     grads = pltpu.with_memory_space_constraint(grads, pltpu.VMEM)
-    partial = project(grads, first_moment_estimate, second_moment_estimate, seeds, grp, held)
+    partial = project(grads, first_moment_estimate, second_moment_estimate, seeds, grp, held, early)
     partial = partial.reshape(devices, own_seqs, K // LANES, LANES)
     partial = lax.all_to_all(partial, AXES, 0, 0, tiled=True)
+    partial = pltpu.with_memory_space_constraint(partial, pltpu.VMEM)
     out = pl.pallas_call(
         finish_kernel,
         out_shape=jax.ShapeDtypeStruct((own_seqs, K // LANES, LANES), jnp.float32),
+        in_specs=[pl.BlockSpec(memory_space=pltpu.VMEM)],
+        compiler_params=pltpu.CompilerParams(vmem_limit_bytes=FINISH_VMEM),
         name="finish",
     )(partial)
     return out.reshape(own_seqs, K)

time: 126 us -> 127 us (level)
  Pallas kernels: 101 us -> 103 us
    pallas_call x1, Pallas kernels: 61.2 us -> 63.1 us  [project(): pl.pallas_call(project_kernel, out_shape=jax.ShapeDtypeStruct((seqs * fea...]
where the time goes in v7:
time: 127 us
  Pallas kernels  103 us (81%)
  blocking collectives  16.1 us (13%)
  starting transfers between devices  7.34 us (6%)
    pallas_call x1, Pallas kernels, project(): pl.pallas_call(project_kernel, out_shape=jax.ShapeDtypeStruct((seqs * fea...  63.1 us
    pallas_call x1, Pallas kernels, presign(): pl.pallas_call(functools.partial(presign_kernel, rows=rows, halves=cols /...  27.7 us
    all_to_all x1, blocking collectives, shards(): partial = lax.all_to_all(partial, AXES, 0, 0, tiled=True)  16.1 us
    pallas_call x1, Pallas kernels, seq_grads(): pl.pallas_call(functools.partial(grad_kernel, single=seqs == 1), out_shap...  11.1 us
    all_to_all x1, starting transfers between devices, shards(): lax.all_to_all(grads, AXES, 0, 0, tiled=True)  7.34 us
  transfers between devices with their start and end apart: 1, of which 0 were waited for; matrix products, arithmetic and copies ran while one was open for 0% of the time, Pallas kernels for 22%

profile of v7, /device:TPU:0, one launch (start us, length us, event | category | flops | bytes accessed | tf_op | source)
XLA Modules:
  0.0 126.8 jit_solution(13735381215379083934)
XLA Ops:
  0.7 11.1 %seq_grads.1 = (bf16[2,16,1,32,512]{4,3,2,1,0:T(8,128)(2,1)}, s32[2,16,256,128]{3,2,1,0:T(8,128)}) custom-call(s32[1]{0:T(128)S(6)} %copy.9.lens_ref, s32[8]{0:T(128)} %seeds_ref.5, s32[1]{0:T(128)} %bitcast.grp_ref, bf16[64,8192]{1,0:T(8,128)(2,1)} %bitcast.10, bf16[1,256,8192]{2,1,0:T(8,128)(2,1)} %outg_any.1, bf16[1,256,8192]{2,1,0:T(8,128)(2,1)} %hid_any.1), custom_call_target="tpu_custom_call" | custom-call | tf_op jit(solution)/shard_map/seq_grads/pallas_call | solution.py:152
  11.8 7.3 %all-to-all-start = ((bf16[32,1,32,512]{3,2,1,0:T(8,128)(2,1)}), bf16[32,1,32,512]{3,2,1,0:T(8,128)(2,1)S(1)}, u32[]{:S(2)}, u32[]{:S(2)}) async-start(bf16[32,1,32,512]{3,2,1,0:T(8,128)(2,1)} %bitcast.11), calls=%async_computation | async-start | bytes 2097152 | tf_op jit(solution)/shard_map/all_to_all | solution.py:446
  19.1 27.7 %presign.1.held_any = s32[10,32,256,128]{3,2,1,0:T(8,128)} custom-call(s32[8]{0:T(128)} %seeds_ref.5, s32[1]{0:T(128)} %bitcast.grp_ref), custom_call_target="tpu_custom_call" | custom-call | flops 209715200 | bytes 41943040 | tf_op jit(solution)/shard_map/presign/pallas_call | solution.py:254
  46.8 0.0 all-to-all-done
  46.8 63.1 %project.1 = bf16[1024,128]{1,0:T(8,128)(2,1)} custom-call(s32[8]{0:T(128)} %seeds_ref.5, s32[1]{0:T(128)} %bitcast.grp_ref, bf16[32,32,512]{2,1,0:T(8,128)(2,1)S(1)} %bitcast.8, f32[64,512]{1,0:T(8,128)} %first_ref.1, f32[64,512]{1,0:T(8,128)} %second_ref.1, s32[10,32,256,128]{3,2,1,0:T(8,128)} %presign.1.held_any, ...), custom_call_target="tpu_custom_call" | custom-call | tf_op jit(solution)/shard_map/project/pallas_call | solution.py:391
  109.9 16.1 %all_to_all.10.partial_ref = bf16[32,1,32,128]{3,2,1,0:T(8,128)(2,1)S(1)} all-to-all(bf16[32,1,32,128]{3,2,1,0:T(8,128)(2,1)} %bitcast.9), channel_id=1, replica_groups=mesh['grp'=2,'wide'=16] {'grp','wide'}, dimensions={0} | all-to-all | bytes 524288 | tf_op jit(solution)/shard_map/all_to_all | solution.py:450
  126.0 0.7 finish.1
Async XLA Ops:
  11.8 35.0 %all-to-all-start = ((bf16[32,1,32,512]{3,2,1,0:T(8,128)(2,1)}), bf16[32,1,32,512]{3,2,1,0:T(8,128)(2,1)S(1)}, u32[]{:S(2)}, u32[]{:S(2)}) async-start(bf16[32,1,32,512]{3,2,1,0:T(8,128)(2,1)} %bitcast.11), calls=%async_computation | async-start | bytes 2097152 | tf_op jit(solution)/shard_map/all_to_all | solution.py:446

commit v8 on v6

--- a/solution.py
+++ b/solution.py
@@ -22,7 +22,7 @@
 SEQ_BLOCK = 16
 PROJECT_VMEM = 36 << 20
 FINISH_VMEM = 8 << 20
-HALVES = 2
+HALVES = 1
 
 
 def shift_down(bits, places):

time: 125 us -> 125 us (level)
  no operation moved by 1% of the time
where the time goes in v8:
time: 125 us; the launch traced here: 124 us
  Pallas kernels  100 us (80%)
  blocking collectives  15.9 us (13%)
  starting transfers between devices  7.34 us (6%)
    pallas_call x1, Pallas kernels, project(): pl.pallas_call(project_kernel, out_shape=jax.ShapeDtypeStruct((seqs * fea...  61.2 us
    pallas_call x1, Pallas kernels, presign(): pl.pallas_call(functools.partial(presign_kernel, rows=rows, halves=cols /...  27.8 us
    all_to_all x1, blocking collectives, shards(): partial = lax.all_to_all(partial, AXES, 0, 0, tiled=True)  15.9 us
    pallas_call x1, Pallas kernels, seq_grads(): pl.pallas_call(functools.partial(grad_kernel, single=seqs == 1), out_shap...  10.7 us
    all_to_all x1, starting transfers between devices, shards(): lax.all_to_all(grads, AXES, 0, 0, tiled=True)  7.34 us
  transfers between devices with their start and end apart: 1, of which 0 were waited for; matrix products, arithmetic and copies ran while one was open for 0% of the time, Pallas kernels for 22%

profile of v8, /device:TPU:0, one launch (start us, length us, event | category | flops | bytes accessed | tf_op | source)
XLA Modules:
  0.0 124.4 jit_solution(6345957141514125401)
XLA Ops:
  0.7 10.7 %seq_grads.1 = (bf16[2,16,1,32,512]{4,3,2,1,0:T(8,128)(2,1)}, s32[12,32,256,128]{3,2,1,0:T(8,128)}) custom-call(s32[1]{0:T(128)S(6)} %copy.11.lens_ref, s32[8]{0:T(128)} %seeds_ref.5, s32[1]{0:T(128)} %bitcast.grp_ref, bf16[64,8192]{1,0:T(8,128)(2,1)} %bitcast.10, bf16[1,256,8192]{2,1,0:T(8,128)(2,1)} %outg_any.1, bf16[1,256,8192]{2,1,0:T(8,128)(2,1)} %hid_any.1), custom_call_target="tpu_custom_call" | custom-call | tf_op jit(solution)/shard_map/seq_grads/pallas_call | solution.py:149
  11.3 7.3 %all-to-all-start = ((bf16[32,1,32,512]{3,2,1,0:T(8,128)(2,1)}), bf16[32,1,32,512]{3,2,1,0:T(8,128)(2,1)S(1)}, u32[]{:S(2)}, u32[]{:S(2)}) async-start(bf16[32,1,32,512]{3,2,1,0:T(8,128)(2,1)} %bitcast.11), calls=%async_computation | async-start | bytes 2097152 | tf_op jit(solution)/shard_map/all_to_all | solution.py:426
  18.7 0.0 copy-start
  18.7 0.0 copy-start.1
  18.7 0.0 copy-start.2
  18.7 27.8 %presign.1.held_any = s32[12,32,256,128]{3,2,1,0:T(8,128)} custom-call(s32[8]{0:T(128)} %seeds_ref.5, s32[1]{0:T(128)} %bitcast.grp_ref, s32[12,32,256,128]{3,2,1,0:T(8,128)} %get-tuple-element.8.early_ref), custom_call_target="tpu_custom_call", output_to_operand_aliasing={{}: (2, {})} | custom-call | flops 251658240 | bytes 50331648 | tf_op jit(solution)/shard_map/presign/pallas_call | solution.py:245
  46.5 0.0 all-to-all-done
  46.5 0.0 copy-done
  46.5 0.0 copy-done.1
  46.5 0.0 copy-done.2
  46.5 61.2 %project.1 = bf16[1024,128]{1,0:T(8,128)(2,1)S(1)} custom-call(s32[8]{0:T(128)S(1)} %copy-done.2, s32[1]{0:T(128)} %bitcast.grp_ref, bf16[32,32,512]{2,1,0:T(8,128)(2,1)S(1)} %bitcast.8, f32[64,512]{1,0:T(8,128)S(1)} %copy-done, f32[64,512]{1,0:T(8,128)S(1)} %copy-done.1, s32[12,32,256,128]{3,2,1,0:T(8,128)} %presign.1.held_any), custom_call_target="tpu_custom_call" | custom-call | tf_op jit(solution)/shard_map/project/pallas_call | solution.py:374
  107.8 15.9 %all_to_all.10.partial_ref = bf16[32,1,32,128]{3,2,1,0:T(8,128)(2,1)S(1)} all-to-all(bf16[32,1,32,128]{3,2,1,0:T(8,128)(2,1)S(1)} %bitcast.9), channel_id=1, replica_groups=mesh['grp'=2,'wide'=16] {'grp','wide'}, dimensions={0} | all-to-all | bytes 524288 | tf_op jit(solution)/shard_map/all_to_all | solution.py:430
  123.7 0.7 finish.1
Async XLA Ops:
  11.3 35.2 %all-to-all-start = ((bf16[32,1,32,512]{3,2,1,0:T(8,128)(2,1)}), bf16[32,1,32,512]{3,2,1,0:T(8,128)(2,1)S(1)}, u32[]{:S(2)}, u32[]{:S(2)}) async-start(bf16[32,1,32,512]{3,2,1,0:T(8,128)(2,1)} %bitcast.11), calls=%async_computation | async-start | bytes 2097152 | tf_op jit(solution)/shard_map/all_to_all | solution.py:426
  18.7 27.9 %copy-start = (f32[64,512]{1,0:T(8,128)S(1)}, f32[64,512]{1,0:T(8,128)}, u32[]{:S(2)}) copy-start(f32[64,512]{1,0:T(8,128)} %first_ref.1) | copy-start | bytes 393220
  18.7 27.8 %copy-start.1 = (f32[64,512]{1,0:T(8,128)S(1)}, f32[64,512]{1,0:T(8,128)}, u32[]{:S(2)}) copy-start(f32[64,512]{1,0:T(8,128)} %second_ref.1) | copy-start | bytes 393220
  18.7 27.8 %copy-start.2 = (s32[8]{0:T(128)S(1)}, s32[8]{0:T(128)}, u32[]{:S(2)}) copy-start(s32[8]{0:T(128)} %seeds_ref.5) | copy-start | bytes 100
